TPU v7x, 512 devices: a whole 4x4x16 slice. The times are simulated.
512 devices in a mesh: grp: 32 (over y, x, core), sub: 16 (over z).
Axes of the slice: x: 4, y: 4, z: 16, core: 2. Of those that a mesh axis runs over, the one named last changes fastest.
Arguments:
- loads: bfloat16 [32, 16, 16, 1536], P('grp', 'sub'), may hold values from -6 to 6
- boundary_values: float32 [16, 6144], replicated, may hold values from -6 to 6
- dirichlet_ids: int32 [32, 16, 3, 128], P('grp', 'sub'), may hold values from 0 to 6143
- dirichlet_coupling: bfloat16 [32, 16, 3, 512, 128], P('grp', 'sub'), may hold values from -0.5 to 0.5
- local_inverse: bfloat16 [32, 16, 3, 512, 512], P('grp', 'sub'), as said below
- local_schur: bfloat16 [32, 16, 3, 512, 512], P('grp', 'sub')
- corner_coupling: bfloat16 [32, 16, 3, 24, 512], P('grp', 'sub'), may hold values from -0.25 to 0.25
- corner_ids: int32 [32, 16, 3, 24], P('grp', 'sub'), may hold values from 0 to 12287
- coarse_inverse: bfloat16 [12288, 12288], P(('grp', 'sub')), as said below
- row_counts: int32 [32, 16, 18], P('grp', 'sub'), may hold values from 0 to 256, as said below
- slot_of: int32 [32, 16, 1536], P('grp', 'sub'), may hold values from 0 to 1535, each once within a row
Outputs:
- multipliers: float32 [32, 16, 16, 1536], P('grp', 'sub')
- residual: float32 [32, 16, 16, 1536], P('grp', 'sub')
Inputs may be any that keep to these rules, and one draw needn't show every extreme that they name: row_counts[g, s, p] for p < 16 equals row_counts[g, p, s], is 0 for p = s and lies in 1 to 64 otherwise; every device reaches 64 with some peer. Column 16 of device (g, s) equals column 17 of device (g - 1, s), lies in 1 to 256, reaches 256 on some device of every slab boundary, and is 0 in the first slab; column 17 is 0 in the last slab. coarse_inverse is symmetric and positive definite. local_inverse and local_schur are symmetric and positive definite.
All inputs are finite; a program needn't handle non-finite values.
Results may differ from a plain program's by a relative error of at most 0.012.
Values may be sent and summed in bfloat16 or wider, within the bound.
No kernel may reach another device: no remote copies, remote signals or barrier semaphores. Data moves between devices by JAX's collectives and lax.ppermute only.
A program may use at most 64 MiB of HBM per device.

v0:
```python
import jax
import jax.numpy as jnp
from jax import lax
from jax.experimental import pallas as pl
from jax.experimental.pallas import tpu as pltpu
from jax.sharding import PartitionSpec as P


IFACE = 512
SUBS = 3
LOADS = 16
CORNERS = 24
FIXED = 128
SLAB = 256
PEER = 64
N_GRP = 32
N_SUB = 16
LENGTH = SUBS * IFACE
WITHIN = N_SUB * PEER
LANES = 128
COARSE = 12288
ROWS = COARSE // N_GRP
COLS = COARSE // N_SUB
OWN = SUBS * CORNERS
BOUNDARY = 6144
F32 = jnp.float32
BF16 = jnp.bfloat16
VMEM_LIMIT = 48 * 1024 * 1024
OH_PARTS = 8
PICK_PARTS = 4
FIELD_PARTS = 6


def nt(a, b):
    return lax.dot_general(a, b, (((1,), (1,)), ((), ())), preferred_element_type=F32)


def nn(a, b):
    return jnp.dot(a, b, preferred_element_type=F32)


def iota(shape, dim):
    return lax.broadcasted_iota(jnp.int32, shape, dim)


def onehot(test):
    return jnp.where(test, 1.0, 0.0).astype(BF16)


def roll(x, shift):
    return pltpu.roll(x, shift, 1)


def call(body, outs, *args, smem=(), hbm=(), out_hbm=(), scratch=()):
    def place(i, chosen):
        if i in chosen:
            return pl.BlockSpec(memory_space=pltpu.HBM)
        return pl.BlockSpec(memory_space=pltpu.VMEM)

    specs = [
        pl.BlockSpec(memory_space=pltpu.SMEM) if i in smem else place(i, hbm) for i in range(len(args))
    ]
    args = [
        pltpu.with_memory_space_constraint(x, pltpu.HBM) if i in hbm else x for i, x in enumerate(args)
    ]
    return pl.pallas_call(
        body,
        out_shape=[
            pltpu.HBM(s, d) if i in out_hbm else jax.ShapeDtypeStruct(s, d)
            for i, (s, d) in enumerate(outs)
        ],
        in_specs=specs,
        out_specs=[place(i, out_hbm) for i in range(len(outs))],
        scratch_shapes=list(scratch),
        compiler_params=pltpu.CompilerParams(vmem_limit_bytes=VMEM_LIMIT),
    )(*args)


def started(pairs, sems):
    copies = [pltpu.make_async_copy(src, dst, sems.at[i]) for i, (src, dst) in enumerate(pairs)]
    for copy in copies:
        copy.start()
    return copies


def live_mask(counts):
    lane = iota((LOADS, LANES), 1)
    parts = []
    for k in range(N_SUB // 2):
        limit = jnp.where(lane < PEER, counts[0, 2 * k], counts[0, 2 * k + 1] + PEER)
        parts.append(lane < limit)
    for side in range(2):
        for half in range(2):
            parts.append(lane + LANES * half < counts[0, N_SUB + side])
    return [jnp.where(p, 1.0, 0.0) for p in parts]


def pack(y, peers, below, above):
    low = iota((8, LANES), 1) < PEER
    for k in range(N_SUB // 2):
        block = y[:, LANES * k : LANES * (k + 1)]
        top, bottom = block[:8], block[8:]
        peers[2 * k] = jnp.where(low, top, roll(bottom, PEER))
        peers[2 * k + 1] = jnp.where(low, roll(top, PEER), bottom)
    below[...] = y[:, WITHIN : WITHIN + SLAB]
    above[...] = y[:, WITHIN + SLAB :]


def unpack(peers, from_below, from_above):
    low = iota((8, LANES), 1) < PEER
    parts = []
    for k in range(N_SUB // 2):
        m, n = peers[2 * k], peers[2 * k + 1]
        top = jnp.where(low, m, roll(n, PEER))
        bottom = jnp.where(low, roll(m, PEER), n)
        parts.append(jnp.concatenate([top, bottom], axis=0))
    for ref in (from_below, from_above):
        parts += [ref[:, :LANES], ref[:, LANES:]]
    return parts


def jump(y, peers, from_below, from_above, counts, scale):
    masks = live_mask(counts)
    other = unpack(peers, from_below, from_above)
    parts = []
    for k in range(LENGTH // LANES):
        own = y[:, LANES * k : LANES * (k + 1)]
        parts.append(scale * masks[k] * (own - other[k]))
    return jnp.concatenate(parts, axis=1)


def split3(x):
    hi = x.astype(BF16)
    rest = x - hi.astype(F32)
    mid = rest.astype(BF16)
    low = (rest - mid.astype(F32)).astype(BF16)
    return hi, mid, low


def spread(x):
    hi, mid, low = (part.astype(F32) for part in split3(x))
    return hi + roll(mid, 8) + roll(low, 16)


def gathered(x):
    return x + roll(x, LANES - 8) + roll(x, LANES - 16)


def dot_rows(a, b):
    return jnp.sum(a * b, axis=1, keepdims=True)


def k_setup(
    bv_hbm, dids_hbm, dc_hbm, loads_hbm, slots_hbm, corner_hbm, ids, counts,
    u_out, chat_out, x_out, msg,
    bv, dids, dc, loads, slots, corner, u_buf, sems, out_sems,
):
    step = 768
    sources = (slots_hbm, dids_hbm, bv_hbm, corner_hbm, dc_hbm, loads_hbm)
    waits = started(tuple(zip(sources, (slots, dids, bv, corner, dc, loads))), sems)
    waits[0].wait()
    moves = []
    for a in range(SUBS):
        rows = slice(IFACE * a, IFACE * (a + 1))
        u_buf[rows, :] = onehot(iota((IFACE, LENGTH), 0) + IFACE * a == slots[...])
        moves.append(pltpu.make_async_copy(u_buf.at[rows, :], u_out.at[rows, :], out_sems.at[a]))
        moves[-1].start()
    for wait in waits[1:]:
        wait.wait()
    picked = jnp.zeros((LOADS, SUBS * FIXED), F32)
    for i in range(BOUNDARY // step):
        oh = onehot(iota((step, SUBS * FIXED), 0) + step * i == dids[...])
        picked += nn(bv[:, step * i : step * (i + 1)].astype(BF16), oh)
    picked = picked.astype(BF16)
    x = jnp.zeros((LOADS, LENGTH), F32)
    chat = []
    for a in range(SUBS):
        lifted = nt(picked[:, FIXED * a : FIXED * (a + 1)], dc[a])
        raw = (loads[:, IFACE * a : IFACE * (a + 1)].astype(F32) - lifted).astype(BF16)
        u = u_buf[IFACE * a : IFACE * (a + 1), :]
        x += nn(raw, u)
        chat.append(nn(corner[a], u))
    masks = live_mask(counts)
    x = jnp.concatenate(
        [masks[k] * x[:, LANES * k : LANES * (k + 1)] for k in range(LENGTH // LANES)], axis=1
    ).astype(BF16)
    x_out[...] = x
    chat.append(jnp.zeros((LANES - OWN, LENGTH), F32))
    chat = jnp.concatenate(chat, axis=0).astype(BF16)
    chat_out[...] = chat
    terms = nt(x, chat)
    row = iota((8, LANES), 0)
    high = jnp.broadcast_to(lax.shift_right_arithmetic(ids[...], 7), (8, LANES)).astype(F32)
    low = jnp.broadcast_to(jnp.bitwise_and(ids[...], 127), (8, LANES)).astype(F32)
    table = jnp.where(row == 0, high, jnp.where(row == 1, low, 0.0))
    tile = jnp.concatenate([terms, table], axis=0).astype(BF16)
    for g in range(N_GRP):
        msg[g] = tile
    for move in moves:
        move.wait()


def id_row(tile):
    tile = tile.astype(F32)
    return (tile[0:1] * 128.0 + tile[1:2]).astype(jnp.int32)


def k_load_first(recv, ids, where, oh_out, msg, oh_buf, sems):
    moves = []
    base = where[0, 0] * ROWS
    load = jnp.zeros((LOADS, ROWS), F32)
    for j in range(N_GRP // 2):
        pair = [recv[2 * j + i] for i in range(2)]
        row = jnp.concatenate([id_row(t[LOADS:]) for t in pair], axis=1)
        oh = onehot(iota((ROWS, 2 * LANES), 0) + base == row)
        oh_buf[j // 2, :, 2 * LANES * (j % 2) : 2 * LANES * (j % 2 + 1)] = oh
        if j % 2:
            moves.append(pltpu.make_async_copy(oh_buf.at[j // 2], oh_out.at[j // 2], sems.at[j // 2]))
            moves[-1].start()
        load += nt(jnp.concatenate([t[:LOADS] for t in pair], axis=1), oh)
    row = iota((8, LANES), 0)
    high = jnp.broadcast_to(lax.shift_right_arithmetic(ids[...], 7), (8, LANES)).astype(F32)
    low = jnp.broadcast_to(jnp.bitwise_and(ids[...], 127), (8, LANES)).astype(F32)
    table = jnp.where(row == 0, high, jnp.where(row == 1, low, 0.0))
    table = jnp.concatenate([table, jnp.zeros((8, ROWS - LANES), F32)], axis=1)
    tile = jnp.concatenate([load, table], axis=0).astype(BF16)
    for p in range(N_SUB):
        msg[p] = tile
    for move in moves:
        move.wait()


def k_load(recv, oh_hbm, msg, oh, sems):
    waits = started([(oh_hbm.at[i], oh.at[i]) for i in range(OH_PARTS)], sems)
    load = jnp.zeros((LOADS, ROWS), F32)
    for i, wait in enumerate(waits):
        terms = jnp.concatenate([recv[4 * i + g] for g in range(4)], axis=1)
        wait.wait()
        load += nt(terms, oh[i])
    load = load.astype(BF16)
    for p in range(N_SUB):
        msg[p] = load


def k_pick_table(recv, where, oh_out, oh_buf, sems):
    moves = []
    base = where[0, 1] * CORNERS
    dof = jnp.concatenate(
        [iota((CORNERS, LANES), 0) + (base + ROWS * g) for g in range(N_GRP)], axis=0
    )
    for p in range(N_SUB):
        row = id_row(recv[p, LOADS : LOADS + 8, :LANES])
        oh_buf[p // 4, :, LANES * (p % 4) : LANES * (p % 4 + 1)] = onehot(dof == row)
        if p % 4 == 3:
            moves.append(pltpu.make_async_copy(oh_buf.at[p // 4], oh_out.at[p // 4], sems.at[p // 4]))
            moves[-1].start()
    for move in moves:
        move.wait()


def slab_load(recv):
    total = recv[0, :LOADS, :].astype(F32)
    for p in range(1, N_SUB):
        total += recv[p, :LOADS, :].astype(F32)
    return total


def halves(x):
    hi = x.astype(BF16)
    return jnp.concatenate([hi, (x - hi.astype(F32)).astype(BF16)], axis=0)


def joined(x):
    if x.shape[0] == LOADS:
        return x[...]
    return x[:LOADS] + x[LOADS:]


def k_solve(recv, block, msg):
    values = joined(nt(halves(slab_load(recv)), block[...])).astype(BF16)
    for g in range(N_GRP):
        msg[g] = values


def k_solve_last(recv, block, gram, field, local, where, msg):
    load = slab_load(recv)
    values = joined(nt(halves(load), block[...])).astype(BF16)
    energy = dot_rows(field[...], joined(local))
    lane = iota((LOADS, LANES), 1)
    sums = roll(spread(jnp.where(lane == 4, energy, gram[...])), CORNERS)
    chunk = jnp.zeros((LOADS, LANES), F32)
    for s in range(N_SUB):
        piece = load[:, CORNERS * s : CORNERS * (s + 1)]
        piece = jnp.concatenate([piece, jnp.zeros((LOADS, LANES - CORNERS), F32)], axis=1)
        chunk = jnp.where(where[0, 1] == s, piece, chunk)
    sums = jnp.where(lane < CORNERS, chunk, sums)
    tile = jnp.concatenate([values, sums.astype(BF16)], axis=1)
    for g in range(N_GRP):
        msg[g] = tile


def coarse_sum(recv, start, size):
    total = recv[0, :, start : start + size].astype(F32)
    for g in range(1, N_GRP):
        total += recv[g, :, start : start + size].astype(F32)
    return total


def pick_starts(oh_hbm, oh, sems):
    return started([(oh_hbm.at[i], oh.at[i]) for i in range(PICK_PARTS)], sems)


def k_pick(recv, oh_hbm, msg, oh, sems):
    waits = pick_starts(oh_hbm, oh, sems)
    values = coarse_sum(recv, 0, COLS).astype(BF16)
    for i, wait in enumerate(waits):
        wait.wait()
        picked = nn(values, oh[i]).astype(BF16)
        for p in range(4):
            msg[4 * i + p] = picked[:, LANES * p : LANES * (p + 1)]


def k_pick_last(recv, oh_hbm, msg, oh, sems):
    waits = pick_starts(oh_hbm, oh, sems)
    values = coarse_sum(recv, 0, COLS)
    lane = iota((LOADS, LANES), 1)
    sums = jnp.where(lane < CORNERS, 0.0, coarse_sum(recv, COLS, LANES))
    sums = gathered(roll(sums, LANES - CORNERS))
    load = [recv[g, :, COLS : COLS + CORNERS].astype(F32) for g in range(N_GRP)]
    energy = dot_rows(jnp.concatenate(load, axis=1), values)
    sums = jnp.where(lane == 5, energy, jnp.where(lane < 5, sums, 0.0))
    sums = roll(spread(sums), OWN)
    values = values.astype(BF16)
    for i, wait in enumerate(waits):
        wait.wait()
        picked = nn(values, oh[i])
        for p in range(4):
            msg[4 * i + p] = (picked[:, LANES * p : LANES * (p + 1)] + sums).astype(BF16)


def corner_sum(recv):
    total = recv[0].astype(F32)
    for p in range(1, N_SUB):
        total += recv[p].astype(F32)
    return total


def k_correct(recv, chat, local, y_out, peers, below, above):
    y = joined(local) + nn(corner_sum(recv).astype(BF16), chat[...])
    y_out[...] = y
    pack(y, peers, below, above)


def k_correct_last(recv, chat, local, y_out, peers, below, above, sums_out):
    total = corner_sum(recv)
    lane = iota((LOADS, LANES), 1)
    at_corners = jnp.where(lane < OWN, total, 0.0).astype(BF16)
    y = joined(local) + nn(at_corners, chat[...])
    y_out[...] = y
    pack(y, peers, below, above)
    sums_out[...] = gathered(roll(jnp.where(lane < OWN, 0.0, total), LANES - OWN))


def k_smooth(y, peers, lo, hi, counts, schur_hbm, r_out, m_out, peers_out, below, above, schur, sems):
    rows = [slice(SLAB * i, SLAB * (i + 1)) for i in range(FIELD_PARTS)]
    waits = started([(schur_hbm.at[part, :], schur.at[part, :]) for part in rows], sems)
    r = jump(y, peers, lo, hi, counts, 1.0)
    r_out[...] = r
    r = halves(r)
    m = jnp.zeros((2 * LOADS, LENGTH), F32)
    for part, wait in zip(rows, waits):
        wait.wait()
        m += nn(r[:, part], schur[part, :])
    m = joined(m)
    m_out[...] = m
    pack(m, peers_out, below, above)


def k_search(m, peers, lo, hi, counts, chat, x_out, b_out, msg):
    x = jump(m, peers, lo, hi, counts, 0.25)
    x_out[...] = x
    b = halves(x)
    b_out[...] = b
    terms = joined(nt(b, chat[...])).astype(BF16)
    for g in range(N_GRP):
        msg[g] = terms


def k_search_last(m, peers, lo, hi, counts, chat, r0, p0, q0, x_out, b_out, gram_out, msg):
    w = jump(m, peers, lo, hi, counts, 0.25)
    x_out[...] = w
    b = halves(w)
    b_out[...] = b
    terms = joined(nt(b, chat[...])).astype(BF16)
    for g in range(N_GRP):
        msg[g] = terms
    r, p, q = r0[...], p0[...], q0[...]
    lane = iota((LOADS, LANES), 1)
    gram = jnp.zeros((LOADS, LANES), F32)
    for i, pair in enumerate(((r, p), (p, q), (r, w), (q, w))):
        gram = jnp.where(lane == i, dot_rows(*pair), gram)
    gram_out[...] = gram


def k_finish(
    y, peers, lo, hi, counts, sums, r0, p0, q0, w0, u_hbm, mult_out, res_out, u, sems
):
    rows = [slice(SLAB * i, SLAB * (i + 1)) for i in range(FIELD_PARTS)]
    waits = started([(u_hbm.at[part, :], u.at[part, :]) for part in rows], sems)
    z = jump(y, peers, lo, hi, counts, 1.0)
    rp, pq, rw, qw, local, coarse = (sums[:, i : i + 1] for i in range(6))
    p, q, w = p0[...], q0[...], w0[...]
    first = rp / pq
    inner = rp - first * (rw + pq) + first * first * qw
    grow = 1.0 + inner / rp
    curvature = grow * grow * pq - 2.0 * grow * first * qw + 2.0 * first * first * (local + coarse)
    second = inner / curvature
    mult = first * p + second * (grow * p - first * w)
    res = r0[...] - first * q - second * (grow * q - first * z)
    stacked = jnp.concatenate(list(split3(mult)) + list(split3(res)), axis=0)
    for part, wait in zip(rows, waits):
        wait.wait()
        placed = nt(stacked, u[part, :])
        mult_out[:, part] = placed[0:16] + placed[16:32] + placed[32:48]
        res_out[:, part] = placed[48:64] + placed[64:80] + placed[80:96]


def k_columns(rows, out):
    for g in range(N_GRP):
        out[g] = rows[:, ROWS * g : ROWS * (g + 1)]


def k_permute(u, blocks, out):
    columns = pl.ds(pl.multiple_of(pl.program_id(0) * IFACE, IFACE), IFACE)
    total = jnp.zeros((IFACE, LENGTH), F32)
    for a in range(SUBS):
        rows = slice(IFACE * a, IFACE * (a + 1))
        half = lax.dot_general(
            u[rows, columns], blocks[a], (((0,), (0,)), ((), ())), preferred_element_type=F32
        )
        total += nn(half.astype(BF16), u[rows, :])
    out[...] = total.astype(BF16)


def permuted(u, blocks):
    return pl.pallas_call(
        k_permute,
        grid=(SUBS,),
        out_shape=jax.ShapeDtypeStruct((LENGTH, LENGTH), BF16),
        in_specs=[
            pl.BlockSpec((LENGTH, LENGTH), lambda i: (0, 0)),
            pl.BlockSpec((SUBS, IFACE, IFACE), lambda i: (0, 0, 0)),
        ],
        out_specs=pl.BlockSpec((IFACE, LENGTH), lambda i: (i, 0)),
        compiler_params=pltpu.CompilerParams(vmem_limit_bytes=VMEM_LIMIT),
        name="k_permute",
    )(u, blocks)


FIELD = ((LOADS, LENGTH), F32)
FIELD_B = ((LOADS, LENGTH), BF16)
FIELD_H = ((2 * LOADS, LENGTH), BF16)
OH_LOAD = ((OH_PARTS, ROWS, 4 * LANES), BF16)
OH_PICK = ((PICK_PARTS, COLS, 4 * LANES), BF16)
SQUARE = ((LENGTH, LENGTH), BF16)
PEERS = ((N_SUB, 8, LANES), F32)
SIDE = ((LOADS, SLAB), F32)
TILE = ((LOADS, LANES), F32)
MSG_TERMS = ((N_GRP, LOADS, LANES), BF16)
MSG_LOAD = ((N_SUB, LOADS, ROWS), BF16)
MSG_VALUES = ((N_GRP, LOADS, COLS), BF16)
MSG_CORNERS = ((N_SUB, LOADS, LANES), BF16)


def buffers(kind, parts):
    return (pltpu.VMEM(*kind), pltpu.SemaphoreType.DMA((parts,)))


def over(axis, x):
    return lax.all_to_all(x, axis, split_axis=0, concat_axis=0, tiled=True)


def exchange(peers, below, above):
    up = lax.ppermute(above, "grp", [(i, i + 1) for i in range(N_GRP - 1)])
    down = lax.ppermute(below, "grp", [(i + 1, i) for i in range(N_GRP - 1)])
    return over("sub", peers), up, down


def solve(
    loads,
    boundary_values,
    dirichlet_ids,
    dirichlet_coupling,
    local_inverse,
    local_schur,
    corner_coupling,
    corner_ids,
    coarse_inverse,
    row_counts,
    slot_of,
):
    counts = row_counts[0]
    ids = jnp.pad(corner_ids.reshape(1, OWN), ((0, 0), (0, LANES - OWN)), constant_values=-1)
    where = jnp.stack([lax.axis_index("grp"), lax.axis_index("sub")]).astype(jnp.int32).reshape(1, 2)

    (block,) = call(k_columns, (((N_GRP, CORNERS, ROWS), BF16),), coarse_inverse)
    block = over("grp", block)
    block = block.reshape(COLS, ROWS)

    u, chat, x, msg = call(
        k_setup,
        (
            ((LENGTH, LENGTH), BF16),
            ((LANES, LENGTH), BF16),
            FIELD_B,
            ((N_GRP, LOADS + 8, LANES), BF16),
        ),
        boundary_values,
        dirichlet_ids.reshape(1, SUBS * FIXED),
        dirichlet_coupling[0, 0],
        loads[0, 0],
        slot_of[0],
        corner_coupling[0, 0],
        ids,
        counts,
        smem=(7,),
        hbm=(0, 1, 2, 3, 4, 5),
        out_hbm=(0,),
        scratch=(
            pltpu.VMEM((LOADS, BOUNDARY), F32),
            pltpu.VMEM((1, SUBS * FIXED), jnp.int32),
            pltpu.VMEM((SUBS, IFACE, FIXED), BF16),
            pltpu.VMEM((LOADS, LENGTH), BF16),
            pltpu.VMEM((1, LENGTH), jnp.int32),
            pltpu.VMEM((SUBS, CORNERS, IFACE), BF16),
            pltpu.VMEM((LENGTH, LENGTH), BF16),
            pltpu.SemaphoreType.DMA((6,)),
            pltpu.SemaphoreType.DMA((SUBS,)),
        ),
    )

    inverse = permuted(u, local_inverse[0, 0])
    schur = permuted(u, local_schur[0, 0])

    def local_of(b):
        return jnp.dot(b, inverse, preferred_element_type=F32)

    def smooth(y, got):
        return call(
            k_smooth,
            (FIELD, FIELD, PEERS, SIDE, SIDE),
            y,
            *got,
            counts,
            schur,
            smem=(4,),
            hbm=(5,),
            scratch=buffers(SQUARE, FIELD_PARTS),
        )

    got = over("grp", msg)
    local = local_of(x)
    oh_load, msg = call(
        k_load_first,
        (OH_LOAD, ((N_SUB, LOADS + 8, ROWS), BF16)),
        got,
        ids,
        where,
        smem=(2,),
        out_hbm=(0,),
        scratch=buffers(OH_LOAD, OH_PARTS),
    )
    got = over("sub", msg)
    (oh_pick,) = call(
        k_pick_table,
        (OH_PICK,),
        got,
        where,
        smem=(1,),
        out_hbm=(0,),
        scratch=buffers(OH_PICK, PICK_PARTS),
    )
    (msg,) = call(k_solve, (MSG_VALUES,), got, block)
    got = over("grp", msg)
    (msg,) = call(
        k_pick, (MSG_CORNERS,), got, oh_pick, hbm=(1,), scratch=buffers(OH_PICK, PICK_PARTS)
    )
    got = over("sub", msg)
    y, *parts = call(k_correct, (FIELD, PEERS, SIDE, SIDE), got, chat, local)
    got = exchange(*parts)
    r0, m, *parts = smooth(y, got)
    got = exchange(*parts)

    p0, b, msg = call(k_search, (FIELD, FIELD_H, MSG_TERMS), m, *got, counts, chat, smem=(4,))
    got = over("grp", msg)
    local = local_of(b)
    (msg,) = call(
        k_load, (MSG_LOAD,), got, oh_load, hbm=(1,), scratch=buffers(OH_LOAD, OH_PARTS)
    )
    got = over("sub", msg)
    (msg,) = call(k_solve, (MSG_VALUES,), got, block)
    got = over("grp", msg)
    (msg,) = call(
        k_pick, (MSG_CORNERS,), got, oh_pick, hbm=(1,), scratch=buffers(OH_PICK, PICK_PARTS)
    )
    got = over("sub", msg)
    y, *parts = call(k_correct, (FIELD, PEERS, SIDE, SIDE), got, chat, local)
    got = exchange(*parts)
    q0, m, *parts = smooth(y, got)
    got = exchange(*parts)

    w0, b, gram, msg = call(
        k_search_last,
        (FIELD, FIELD_H, TILE, MSG_TERMS),
        m,
        *got,
        counts,
        chat,
        r0,
        p0,
        q0,
        smem=(4,),
    )
    got = over("grp", msg)
    local = local_of(b)
    (msg,) = call(
        k_load, (MSG_LOAD,), got, oh_load, hbm=(1,), scratch=buffers(OH_LOAD, OH_PARTS)
    )
    got = over("sub", msg)
    wide = ((N_GRP, LOADS, COLS + LANES), BF16)
    (msg,) = call(k_solve_last, (wide,), got, block, gram, w0, local, where, smem=(5,))
    got = over("grp", msg)
    (msg,) = call(
        k_pick_last, (MSG_CORNERS,), got, oh_pick, hbm=(1,), scratch=buffers(OH_PICK, PICK_PARTS)
    )
    got = over("sub", msg)
    y, *parts, sums = call(k_correct_last, (FIELD, PEERS, SIDE, SIDE, TILE), got, chat, local)
    got = exchange(*parts)
    mult, res = call(
        k_finish,
        (FIELD, FIELD),
        y,
        *got,
        counts,
        sums,
        r0,
        p0,
        q0,
        w0,
        u,
        smem=(4,),
        hbm=(10,),
        scratch=buffers(SQUARE, FIELD_PARTS),
    )
    return mult[None, None], res[None, None]


def solution(mesh):
    in_specs = (
        P("grp", "sub", None, None),
        P(),
        P("grp", "sub", None, None),
        P("grp", "sub", None, None, None),
        P("grp", "sub", None, None, None),
        P("grp", "sub", None, None, None),
        P("grp", "sub", None, None, None),
        P("grp", "sub", None, None),
        P(("grp", "sub"), None),
        P("grp", "sub", None),
        P("grp", "sub", None),
    )
    out_specs = (P("grp", "sub", None, None), P("grp", "sub", None, None))
    return jax.shard_map(solve, mesh=mesh, in_specs=in_specs, out_specs=out_specs, check_vma=False)
```

profile of v0, /device:TPU:1, one launch (start us, length us, event | category | flops | bytes accessed | tf_op | source)
XLA Modules:
  0.0 403.0 jit_solution(15742417463148987597)
XLA Ops:
  2.1 5.8 %shard_map.122 = (bf16[1536,1536]{1,0:T(8,128)(2,1)}, bf16[128,1536]{1,0:T(8,128)(2,1)S(1)}, bf16[16,1536]{1,0:T(8,128)(2,1)S(1)}, bf16[32,24,128]{2,1,0:T(8,128)(2,1)}) custom-call(f32[16,6144]{1,0:T(8,128)} %bv_hbm.1, s32[1,384]{1,0:T(1,128)} %bitcast.36, bf16[3,512,128]{2,1,0:T(8,128)(2,1)} %bitcast.32, bf16[16,1536]{1,0:T(8,128)(2,1)} %bitcast.34, ...), custom_call_target="tpu_custom_call" | custom-call | tf_op jit(solution)/shard_map/pallas_call | solution.py:66
  7.9 10.4 %all-to-all-start = ((bf16[32,24,128]{2,1,0:T(8,128)(2,1)}), bf16[32,24,128]{2,1,0:T(8,128)(2,1)S(1)}, u32[]{:S(2)}, u32[]{:S(2)}) async-start(bf16[32,24,128]{2,1,0:T(8,128)(2,1)} %get-tuple-element.40), calls=%async_computation | async-start | bytes 393216 | tf_op jit(solution)/shard_map/all_to_all | solution.py:480
  18.3 1.1 copy-done.2
  19.3 0.9 shard_map.124
  20.2 6.4 %all-to-all-done.recv = bf16[32,24,128]{2,1,0:T(8,128)(2,1)S(1)} async-done(((bf16[32,24,128]{2,1,0:T(8,128)(2,1)}), bf16[32,24,128]{2,1,0:T(8,128)(2,1)S(1)}, u32[]{:S(2)}, u32[]{:S(2)}) %all-to-all-start) | async-done | bytes 196640 | tf_op jit(solution)/shard_map/all_to_all | solution.py:480
  26.6 3.8 all-to-all-start.2
  30.5 2.9 shard_map.123
  33.4 9.1 %all-to-all-done.2 = bf16[32,24,384]{2,1,0:T(8,128)(2,1)S(1)} async-done(((bf16[32,24,384]{2,1,0:T(8,128)(2,1)}), bf16[32,24,384]{2,1,0:T(8,128)(2,1)S(1)}, u32[]{:S(2)}, u32[]{:S(2)}) %all-to-all-start.2) | async-done | bytes 589856 | tf_op jit(solution)/shard_map/all_to_all | solution.py:480
  42.6 27.2 %all_to_all.90.recv = bf16[16,24,384]{2,1,0:T(8,128)(2,1)S(1)} all-to-all(bf16[16,24,384]{2,1,0:T(8,128)(2,1)S(1)} %get-tuple-element.41), channel_id=1, replica_groups=mesh['grp'=32,'sub'=16] {'sub'}, dimensions={0} | all-to-all | bytes 589824 | tf_op jit(solution)/shard_map/all_to_all | solution.py:480
  69.7 1.2 shard_map.125
  70.9 10.5 %all-to-all-start.3 = ((bf16[32,16,768]{2,1,0:T(8,128)(2,1)}), bf16[32,16,768]{2,1,0:T(8,128)(2,1)S(1)}, u32[]{:S(2)}, u32[]{:S(2)}) async-start(bf16[32,16,768]{2,1,0:T(8,128)(2,1)} %shard_map.125), calls=%async_computation.3 | async-start | bytes 1572864 | tf_op jit(solution)/shard_map/all_to_all | solution.py:480
  81.5 1.4 copy-done
  82.9 13.9 %k_permute.2 = bf16[1536,1536]{1,0:T(8,128)(2,1)} custom-call(bf16[1536,1536]{1,0:T(8,128)(2,1)} %get-tuple-element.44.u.u_hbm, bf16[3,512,512]{2,1,0:T(8,128)(2,1)S(1)} %bitcast.24), custom_call_target="tpu_custom_call" | custom-call | tf_op jit(solution)/shard_map/k_permute/pallas_call | solution.py:446
  96.8 2.4 shard_map.126.oh_hbm
  99.2 2.8 shard_map.127
  102.1 5.1 %all-to-all-start.4 = ((bf16[16,16,128]{2,1,0:T(8,128)(2,1)}), bf16[16,16,128]{2,1,0:T(8,128)(2,1)S(1)}, u32[]{:S(2)}, u32[]{:S(2)}) async-start(bf16[16,16,128]{2,1,0:T(8,128)(2,1)} %shard_map.127), calls=%async_computation.4 | async-start | bytes 131072 | tf_op jit(solution)/shard_map/all_to_all | solution.py:480
  107.1 3.1 fusion.local
  110.2 8.5 %all-to-all-done.4.recv = bf16[16,16,128]{2,1,0:T(8,128)(2,1)S(1)} async-done(((bf16[16,16,128]{2,1,0:T(8,128)(2,1)}), bf16[16,16,128]{2,1,0:T(8,128)(2,1)S(1)}, u32[]{:S(2)}, u32[]{:S(2)}) %all-to-all-start.4) | async-done | bytes 65568 | tf_op jit(solution)/shard_map/all_to_all | solution.py:480
  118.7 0.9 shard_map.128
  119.6 4.0 all-to-all-start.5
  123.6 4.9 %collective-permute-start = (f32[16,256]{1,0:T(8,128)S(1)}, f32[16,256]{1,0:T(8,128)S(1)}, u32[]{:S(2)}, u32[]{:S(2)}) collective-permute-start(f32[16,256]{1,0:T(8,128)S(1)} %get-tuple-element.47), channel_id=1, source_target_pairs={{0,16},{16,32},{32,48},{48,64},{64,80},{80,96},{96,112},{112,128},... | collective-permute-start | bytes 49160 | tf_op jit(solution)/shard_map/ppermute | solution.py:484
  128.4 2.1 collective-permute-start.1
  130.6 13.9 %k_permute.3.schur_hbm = bf16[1536,1536]{1,0:T(8,128)(2,1)} custom-call(bf16[1536,1536]{1,0:T(8,128)(2,1)} %get-tuple-element.44.u.u_hbm, bf16[3,512,512]{2,1,0:T(8,128)(2,1)S(1)} %bitcast.25), custom_call_target="tpu_custom_call" | custom-call | tf_op jit(solution)/shard_map/k_permute/pallas_call | solution.py:446
  144.5 3.8 shard_map.129
  148.3 11.7 %all-to-all-start.6 = ((f32[16,8,128]{2,1,0:T(8,128)}), f32[16,8,128]{2,1,0:T(8,128)S(1)}, u32[]{:S(2)}, u32[]{:S(2)}) async-start(f32[16,8,128]{2,1,0:T(8,128)} %get-tuple-element.50), calls=%async_computation.6 | async-start | bytes 131072 | tf_op jit(solution)/shard_map/all_to_all | solution.py:480
  160.0 3.9 collective-permute-start.2
  163.9 1.9 collective-permute-start.3
  165.9 3.4 collective-permute-done.3.hi
  169.3 2.4 all-to-all-done.6.peers
  172.5 16.3 %all_to_all.91.recv = bf16[32,16,128]{2,1,0:T(8,128)(2,1)S(1)} all-to-all(bf16[32,16,128]{2,1,0:T(8,128)(2,1)S(1)} %get-tuple-element.53), channel_id=1, replica_groups=mesh['grp'=32,'sub'=16] {'grp'}, dimensions={0} | all-to-all | bytes 262144 | tf_op jit(solution)/shard_map/all_to_all | solution.py:480
  188.7 2.6 shard_map.131
  191.3 23.2 %all_to_all.92.recv = bf16[16,16,384]{2,1,0:T(8,128)(2,1)S(1)} all-to-all(bf16[16,16,384]{2,1,0:T(8,128)(2,1)S(1)} %shard_map.131), channel_id=1, replica_groups=mesh['grp'=32,'sub'=16] {'sub'}, dimensions={0} | all-to-all | bytes 393216 | tf_op jit(solution)/shard_map/all_to_all | solution.py:480
  214.9 21.5 %all_to_all.93.recv = bf16[32,16,768]{2,1,0:T(8,128)(2,1)S(1)} all-to-all(bf16[32,16,768]{2,1,0:T(8,128)(2,1)S(1)} %shard_map.132), channel_id=1, replica_groups=mesh['grp'=32,'sub'=16] {'grp'}, dimensions={0} | all-to-all | bytes 1572864 | tf_op jit(solution)/shard_map/all_to_all | solution.py:480
  236.4 2.7 shard_map.133
  239.1 5.3 %all-to-all-start.10 = ((bf16[16,16,128]{2,1,0:T(8,128)(2,1)}), bf16[16,16,128]{2,1,0:T(8,128)(2,1)S(1)}, u32[]{:S(2)}, u32[]{:S(2)}) async-start(bf16[16,16,128]{2,1,0:T(8,128)(2,1)} %shard_map.133), calls=%async_computation.10 | async-start | bytes 131072 | tf_op jit(solution)/shard_map/all_to_all | solution.py:480
  244.4 3.2 fusion.1.local
  247.6 8.3 %all-to-all-done.10.recv = bf16[16,16,128]{2,1,0:T(8,128)(2,1)S(1)} async-done(((bf16[16,16,128]{2,1,0:T(8,128)(2,1)}), bf16[16,16,128]{2,1,0:T(8,128)(2,1)S(1)}, u32[]{:S(2)}, u32[]{:S(2)}) %all-to-all-start.10) | async-done | bytes 65568 | tf_op jit(solution)/shard_map/all_to_all | solution.py:480
  256.0 0.9 shard_map.134
  256.8 3.8 all-to-all-start.11
  260.7 4.2 %collective-permute-start.4 = (f32[16,256]{1,0:T(8,128)S(1)}, f32[16,256]{1,0:T(8,128)S(1)}, u32[]{:S(2)}, u32[]{:S(2)}) collective-permute-start(f32[16,256]{1,0:T(8,128)S(1)} %get-tuple-element.58), channel_id=1, source_target_pairs={{0,16},{16,32},{32,48},{48,64},{64,80},{80,96},{96,112},{112,128},... | collective-permute-start | bytes 49160 | tf_op jit(solution)/shard_map/ppermute | solution.py:484
  264.8 1.9 collective-permute-start.5
  266.8 3.4 collective-permute-done.5.hi
  270.2 2.0 all-to-all-done.11.peers
  272.2 3.8 shard_map.135
  276.1 9.3 %all-to-all-start.12 = ((f32[16,8,128]{2,1,0:T(8,128)}), f32[16,8,128]{2,1,0:T(8,128)S(1)}, u32[]{:S(2)}, u32[]{:S(2)}) async-start(f32[16,8,128]{2,1,0:T(8,128)} %get-tuple-element.61), calls=%async_computation.12 | async-start | bytes 131072 | tf_op jit(solution)/shard_map/all_to_all | solution.py:480
  285.4 2.2 collective-permute-start.6
  287.6 2.1 collective-permute-start.7
  289.8 3.2 collective-permute-done.7.hi
  293.0 4.4 %all-to-all-done.12.peers = f32[16,8,128]{2,1,0:T(8,128)S(1)} async-done(((f32[16,8,128]{2,1,0:T(8,128)}), f32[16,8,128]{2,1,0:T(8,128)S(1)}, u32[]{:S(2)}, u32[]{:S(2)}) %all-to-all-start.12) | async-done | bytes 65568 | tf_op jit(solution)/shard_map/all_to_all | solution.py:480
  298.2 14.4 %all_to_all.94.recv = bf16[32,16,128]{2,1,0:T(8,128)(2,1)S(1)} all-to-all(bf16[32,16,128]{2,1,0:T(8,128)(2,1)S(1)} %get-tuple-element.67), channel_id=1, replica_groups=mesh['grp'=32,'sub'=16] {'grp'}, dimensions={0} | all-to-all | bytes 262144 | tf_op jit(solution)/shard_map/all_to_all | solution.py:480
  312.6 3.3 shard_map.137
  315.9 9.5 %all-to-all-start.14 = ((bf16[16,16,384]{2,1,0:T(8,128)(2,1)}), bf16[16,16,384]{2,1,0:T(8,128)(2,1)S(1)}, u32[]{:S(2)}, u32[]{:S(2)}) async-start(bf16[16,16,384]{2,1,0:T(8,128)(2,1)} %shard_map.137), calls=%async_computation.14 | async-start | bytes 393216 | tf_op jit(solution)/shard_map/all_to_all | solution.py:480
  325.3 3.2 fusion.2.local
  328.6 9.4 %all-to-all-done.14.recv = bf16[16,16,384]{2,1,0:T(8,128)(2,1)S(1)} async-done(((bf16[16,16,384]{2,1,0:T(8,128)(2,1)}), bf16[16,16,384]{2,1,0:T(8,128)(2,1)S(1)}, u32[]{:S(2)}, u32[]{:S(2)}) %all-to-all-start.14) | async-done | bytes 196640 | tf_op jit(solution)/shard_map/all_to_all | solution.py:480
  338.8 22.9 %all_to_all.95.recv = bf16[32,16,896]{2,1,0:T(8,128)(2,1)S(1)} all-to-all(bf16[32,16,896]{2,1,0:T(8,128)(2,1)S(1)} %shard_map.138), channel_id=1, replica_groups=mesh['grp'=32,'sub'=16] {'grp'}, dimensions={0} | all-to-all | bytes 1835008 | tf_op jit(solution)/shard_map/all_to_all | solution.py:480
  361.7 2.3 shard_map.139
  364.0 16.6 %all_to_all.96.recv = bf16[16,16,128]{2,1,0:T(8,128)(2,1)S(1)} all-to-all(bf16[16,16,128]{2,1,0:T(8,128)(2,1)S(1)} %shard_map.139), channel_id=1, replica_groups=mesh['grp'=32,'sub'=16] {'sub'}, dimensions={0} | all-to-all | bytes 131072 | tf_op jit(solution)/shard_map/all_to_all | solution.py:480
  380.6 0.9 shard_map.140
  381.5 4.0 all-to-all-start.17
  385.5 4.0 collective-permute-start.8
  389.5 1.9 collective-permute-start.9
  391.4 3.4 collective-permute-done.9.hi
  394.8 2.2 all-to-all-done.17.peers
  397.0 5.8 %shard_map.141 = (f32[16,1536]{1,0:T(8,128)}, f32[16,1536]{1,0:T(8,128)}) custom-call(f32[16,1536]{1,0:T(8,128)S(1)} %get-tuple-element.71.y, f32[16,8,128]{2,1,0:T(8,128)S(1)} %all-to-all-done.17.peers, f32[16,256]{1,0:T(8,128)S(1)} %collective-permute-done.8.lo, f32[16,256]{1,0:T(8,128)S(1)} %collective-permute-done.9.hi, s32[1,18]{1,0:T(1,128)S(1)} %bitcast.31, ...), custom_call_target="tpu_custom_call" | custom-call | tf_op jit(solution)/shard_map/pallas_call | solution.py:66
  (24 shorter events, 4.4 us)
Async XLA Ops:
  1.4 0.7 copy-start.3
  7.9 18.7 %all-to-all-start = ((bf16[32,24,128]{2,1,0:T(8,128)(2,1)}), bf16[32,24,128]{2,1,0:T(8,128)(2,1)S(1)}, u32[]{:S(2)}, u32[]{:S(2)}) async-start(bf16[32,24,128]{2,1,0:T(8,128)(2,1)} %get-tuple-element.40), calls=%async_computation | async-start | bytes 393216 | tf_op jit(solution)/shard_map/all_to_all | solution.py:480
  18.3 1.1 copy-start.2
  26.6 16.0 %all-to-all-start.2 = ((bf16[32,24,384]{2,1,0:T(8,128)(2,1)}), bf16[32,24,384]{2,1,0:T(8,128)(2,1)S(1)}, u32[]{:S(2)}, u32[]{:S(2)}) async-start(bf16[32,24,384]{2,1,0:T(8,128)(2,1)} %shard_map.124), calls=%async_computation.2 | async-start | bytes 1179648 | tf_op jit(solution)/shard_map/all_to_all | solution.py:480
  70.9 28.3 %all-to-all-start.3 = ((bf16[32,16,768]{2,1,0:T(8,128)(2,1)}), bf16[32,16,768]{2,1,0:T(8,128)(2,1)S(1)}, u32[]{:S(2)}, u32[]{:S(2)}) async-start(bf16[32,16,768]{2,1,0:T(8,128)(2,1)} %shard_map.125), calls=%async_computation.3 | async-start | bytes 1572864 | tf_op jit(solution)/shard_map/all_to_all | solution.py:480
  81.5 1.4 copy-start
  99.2 31.4 %copy-start.1 = (bf16[1,1,3,512,512]{4,3,2,1,0:T(8,128)(2,1)S(1)}, bf16[1,1,3,512,512]{4,3,2,1,0:T(8,128)(2,1)}, u32[]{:S(2)}) copy-start(bf16[1,1,3,512,512]{4,3,2,1,0:T(8,128)(2,1)} %param.16) | copy-start | bytes 4718596
  102.1 16.7 %all-to-all-start.4 = ((bf16[16,16,128]{2,1,0:T(8,128)(2,1)}), bf16[16,16,128]{2,1,0:T(8,128)(2,1)S(1)}, u32[]{:S(2)}, u32[]{:S(2)}) async-start(bf16[16,16,128]{2,1,0:T(8,128)(2,1)} %shard_map.127), calls=%async_computation.4 | async-start | bytes 131072 | tf_op jit(solution)/shard_map/all_to_all | solution.py:480
  119.6 24.9 %all-to-all-start.5 = ((f32[16,8,128]{2,1,0:T(8,128)}), f32[16,8,128]{2,1,0:T(8,128)S(1)}, u32[]{:S(2)}, u32[]{:S(2)}) async-start(f32[16,8,128]{2,1,0:T(8,128)} %get-tuple-element.46), calls=%async_computation.5 | async-start | bytes 131072 | tf_op jit(solution)/shard_map/all_to_all | solution.py:480
  123.6 20.9 %collective-permute-start = (f32[16,256]{1,0:T(8,128)S(1)}, f32[16,256]{1,0:T(8,128)S(1)}, u32[]{:S(2)}, u32[]{:S(2)}) collective-permute-start(f32[16,256]{1,0:T(8,128)S(1)} %get-tuple-element.47), channel_id=1, source_target_pairs={{0,16},{16,32},{32,48},{48,64},{64,80},{80,96},{96,112},{112,128},... | collective-permute-start | bytes 49160 | tf_op jit(solution)/shard_map/ppermute | solution.py:484
  128.4 16.0 %collective-permute-start.1 = (f32[16,256]{1,0:T(8,128)S(1)}, f32[16,256]{1,0:T(8,128)S(1)}, u32[]{:S(2)}, u32[]{:S(2)}) collective-permute-start(f32[16,256]{1,0:T(8,128)S(1)} %get-tuple-element.48), channel_id=1, source_target_pairs={{16,0},{32,16},{48,32},{64,48},{80,64},{96,80},{112,96},{128,112},... | collective-permute-start | bytes 49160 | tf_op jit(solution)/shard_map/ppermute | solution.py:485
  130.6 13.9 %copy-start.4 = (s32[1,1,18]{2,1,0:T(1,128)S(1)}, s32[1,1,18]{2,1,0:T(1,128)}, u32[]{:S(2)}) copy-start(s32[1,1,18]{2,1,0:T(1,128)} %param.20) | copy-start | bytes 220
  148.3 23.3 %all-to-all-start.6 = ((f32[16,8,128]{2,1,0:T(8,128)}), f32[16,8,128]{2,1,0:T(8,128)S(1)}, u32[]{:S(2)}, u32[]{:S(2)}) async-start(f32[16,8,128]{2,1,0:T(8,128)} %get-tuple-element.50), calls=%async_computation.6 | async-start | bytes 131072 | tf_op jit(solution)/shard_map/all_to_all | solution.py:480
  160.0 5.9 %collective-permute-start.2 = (f32[16,256]{1,0:T(8,128)S(1)}, f32[16,256]{1,0:T(8,128)S(1)}, u32[]{:S(2)}, u32[]{:S(2)}) collective-permute-start(f32[16,256]{1,0:T(8,128)S(1)} %get-tuple-element.51), channel_id=1, source_target_pairs={{0,16},{16,32},{32,48},{48,64},{64,80},{80,96},{96,112},{112,128},... | collective-permute-start | bytes 49160 | tf_op jit(solution)/shard_map/ppermute | solution.py:484
  163.9 5.4 %collective-permute-start.3 = (f32[16,256]{1,0:T(8,128)S(1)}, f32[16,256]{1,0:T(8,128)S(1)}, u32[]{:S(2)}, u32[]{:S(2)}) collective-permute-start(f32[16,256]{1,0:T(8,128)S(1)} %get-tuple-element.52), channel_id=1, source_target_pairs={{16,0},{32,16},{48,32},{64,48},{80,64},{96,80},{112,96},{128,112},... | collective-permute-start | bytes 49160 | tf_op jit(solution)/shard_map/ppermute | solution.py:485
  239.1 16.8 %all-to-all-start.10 = ((bf16[16,16,128]{2,1,0:T(8,128)(2,1)}), bf16[16,16,128]{2,1,0:T(8,128)(2,1)S(1)}, u32[]{:S(2)}, u32[]{:S(2)}) async-start(bf16[16,16,128]{2,1,0:T(8,128)(2,1)} %shard_map.133), calls=%async_computation.10 | async-start | bytes 131072 | tf_op jit(solution)/shard_map/all_to_all | solution.py:480
  256.8 15.4 %all-to-all-start.11 = ((f32[16,8,128]{2,1,0:T(8,128)}), f32[16,8,128]{2,1,0:T(8,128)S(1)}, u32[]{:S(2)}, u32[]{:S(2)}) async-start(f32[16,8,128]{2,1,0:T(8,128)} %get-tuple-element.57), calls=%async_computation.11 | async-start | bytes 131072 | tf_op jit(solution)/shard_map/all_to_all | solution.py:480
  260.7 6.1 %collective-permute-start.4 = (f32[16,256]{1,0:T(8,128)S(1)}, f32[16,256]{1,0:T(8,128)S(1)}, u32[]{:S(2)}, u32[]{:S(2)}) collective-permute-start(f32[16,256]{1,0:T(8,128)S(1)} %get-tuple-element.58), channel_id=1, source_target_pairs={{0,16},{16,32},{32,48},{48,64},{64,80},{80,96},{96,112},{112,128},... | collective-permute-start | bytes 49160 | tf_op jit(solution)/shard_map/ppermute | solution.py:484
  264.8 5.4 %collective-permute-start.5 = (f32[16,256]{1,0:T(8,128)S(1)}, f32[16,256]{1,0:T(8,128)S(1)}, u32[]{:S(2)}, u32[]{:S(2)}) collective-permute-start(f32[16,256]{1,0:T(8,128)S(1)} %get-tuple-element.59), channel_id=1, source_target_pairs={{16,0},{32,16},{48,32},{64,48},{80,64},{96,80},{112,96},{128,112},... | collective-permute-start | bytes 49160 | tf_op jit(solution)/shard_map/ppermute | solution.py:485
  276.1 21.3 %all-to-all-start.12 = ((f32[16,8,128]{2,1,0:T(8,128)}), f32[16,8,128]{2,1,0:T(8,128)S(1)}, u32[]{:S(2)}, u32[]{:S(2)}) async-start(f32[16,8,128]{2,1,0:T(8,128)} %get-tuple-element.61), calls=%async_computation.12 | async-start | bytes 131072 | tf_op jit(solution)/shard_map/all_to_all | solution.py:480
  285.4 4.3 %collective-permute-start.6 = (f32[16,256]{1,0:T(8,128)S(1)}, f32[16,256]{1,0:T(8,128)S(1)}, u32[]{:S(2)}, u32[]{:S(2)}) collective-permute-start(f32[16,256]{1,0:T(8,128)S(1)} %get-tuple-element.62), channel_id=1, source_target_pairs={{0,16},{16,32},{32,48},{48,64},{64,80},{80,96},{96,112},{112,128},... | collective-permute-start | bytes 49160 | tf_op jit(solution)/shard_map/ppermute | solution.py:484
  287.6 5.4 %collective-permute-start.7 = (f32[16,256]{1,0:T(8,128)S(1)}, f32[16,256]{1,0:T(8,128)S(1)}, u32[]{:S(2)}, u32[]{:S(2)}) collective-permute-start(f32[16,256]{1,0:T(8,128)S(1)} %get-tuple-element.63), channel_id=1, source_target_pairs={{16,0},{32,16},{48,32},{64,48},{80,64},{96,80},{112,96},{128,112},... | collective-permute-start | bytes 49160 | tf_op jit(solution)/shard_map/ppermute | solution.py:485
  315.9 22.1 %all-to-all-start.14 = ((bf16[16,16,384]{2,1,0:T(8,128)(2,1)}), bf16[16,16,384]{2,1,0:T(8,128)(2,1)S(1)}, u32[]{:S(2)}, u32[]{:S(2)}) async-start(bf16[16,16,384]{2,1,0:T(8,128)(2,1)} %shard_map.137), calls=%async_computation.14 | async-start | bytes 393216 | tf_op jit(solution)/shard_map/all_to_all | solution.py:480
  381.5 15.6 %all-to-all-start.17 = ((f32[16,8,128]{2,1,0:T(8,128)}), f32[16,8,128]{2,1,0:T(8,128)S(1)}, u32[]{:S(2)}, u32[]{:S(2)}) async-start(f32[16,8,128]{2,1,0:T(8,128)} %get-tuple-element.72), calls=%async_computation.17 | async-start | bytes 131072 | tf_op jit(solution)/shard_map/all_to_all | solution.py:480
  385.5 5.9 %collective-permute-start.8 = (f32[16,256]{1,0:T(8,128)S(1)}, f32[16,256]{1,0:T(8,128)S(1)}, u32[]{:S(2)}, u32[]{:S(2)}) collective-permute-start(f32[16,256]{1,0:T(8,128)S(1)} %get-tuple-element.73), channel_id=1, source_target_pairs={{0,16},{16,32},{32,48},{48,64},{64,80},{80,96},{96,112},{112,128},... | collective-permute-start | bytes 49160 | tf_op jit(solution)/shard_map/ppermute | solution.py:484
  389.5 5.4 %collective-permute-start.9 = (f32[16,256]{1,0:T(8,128)S(1)}, f32[16,256]{1,0:T(8,128)S(1)}, u32[]{:S(2)}, u32[]{:S(2)}) collective-permute-start(f32[16,256]{1,0:T(8,128)S(1)} %get-tuple-element.74), channel_id=1, source_target_pairs={{16,0},{32,16},{48,32},{64,48},{80,64},{96,80},{112,96},{128,112},... | collective-permute-start | bytes 49160 | tf_op jit(solution)/shard_map/ppermute | solution.py:485
where the time goes:
time: 405 us; the launch traced here: 403 us
  blocking collectives  142 us (35%)
  starting transfers between devices  106 us (26%)
  Pallas kernels  73.6 us (18%)
  waiting for transfers between devices  66.2 us (16%)
  matrix products  9.52 us (2%)
    all_to_all x7, blocking collectives, over(): return lax.all_to_all(x, axis, split_axis=0, concat_axis=0, tiled=True)  142 us
    all_to_all x11, starting transfers between devices, over(): return lax.all_to_all(x, axis, split_axis=0, concat_axis=0, tiled=True)  77.2 us
    all_to_all x11, waiting for transfers between devices, over(): return lax.all_to_all(x, axis, split_axis=0, concat_axis=0, tiled=True)  52.8 us
    pallas_call x20, Pallas kernels, call(): pl.pallas_call(body, out_shape=[pltpu.HBM(s, d) if i in out_hbm else jax....  45.8 us
    pallas_call x2, Pallas kernels, permuted(): pl.pallas_call(k_permute, grid=(SUBS,), out_shape=jax.ShapeDtypeStruct((L...  27.8 us
    ppermute x5, starting transfers between devices, exchange(): up = lax.ppermute(above, 'grp', [(i, i + 1) for i in range(N_GRP - 1)])  19.1 us
    ppermute x5, waiting for transfers between devices, exchange(): down = lax.ppermute(below, 'grp', [(i + 1, i) for i in range(N_GRP - 1)])  13.5 us
    ppermute x5, starting transfers between devices, exchange(): down = lax.ppermute(below, 'grp', [(i + 1, i) for i in range(N_GRP - 1)])  9.97 us
  transfers between devices with their start and end apart: 21, of which 13 were waited for; matrix products, arithmetic and copies ran while one was open for 2% of the time, Pallas kernels for 8%

commit v1 on v0

--- a/solution.py
+++ b/solution.py
@@ -26,7 +26,7 @@
 F32 = jnp.float32
 BF16 = jnp.bfloat16
 VMEM_LIMIT = 48 * 1024 * 1024
-OH_PARTS = 8
+SELECTS = 4
 PICK_PARTS = 4
 FIELD_PARTS = 6
 
@@ -167,11 +167,14 @@
         moves[-1].start()
     for wait in waits[1:]:
         wait.wait()
+
+    def pick(i, total):
+        oh = onehot(iota((step, SUBS * FIXED), 0) + step * i == dids[...])
+        part = bv[:, pl.ds(pl.multiple_of(step * i, step), step)]
+        return total + nn(part.astype(BF16), oh)
+
     picked = jnp.zeros((LOADS, SUBS * FIXED), F32)
-    for i in range(BOUNDARY // step):
-        oh = onehot(iota((step, SUBS * FIXED), 0) + step * i == dids[...])
-        picked += nn(bv[:, step * i : step * (i + 1)].astype(BF16), oh)
-    picked = picked.astype(BF16)
+    picked = lax.fori_loop(0, BOUNDARY // step, pick, picked).astype(BF16)
     x = jnp.zeros((LOADS, LENGTH), F32)
     chat = []
     for a in range(SUBS):
@@ -205,18 +208,13 @@
     return (tile[0:1] * 128.0 + tile[1:2]).astype(jnp.int32)
 
 
-def k_load_first(recv, ids, where, oh_out, msg, oh_buf, sems):
-    moves = []
+def k_load_first(recv, ids, where, msg):
     base = where[0, 0] * ROWS
     load = jnp.zeros((LOADS, ROWS), F32)
     for j in range(N_GRP // 2):
         pair = [recv[2 * j + i] for i in range(2)]
         row = jnp.concatenate([id_row(t[LOADS:]) for t in pair], axis=1)
         oh = onehot(iota((ROWS, 2 * LANES), 0) + base == row)
-        oh_buf[j // 2, :, 2 * LANES * (j % 2) : 2 * LANES * (j % 2 + 1)] = oh
-        if j % 2:
-            moves.append(pltpu.make_async_copy(oh_buf.at[j // 2], oh_out.at[j // 2], sems.at[j // 2]))
-            moves[-1].start()
         load += nt(jnp.concatenate([t[:LOADS] for t in pair], axis=1), oh)
     row = iota((8, LANES), 0)
     high = jnp.broadcast_to(lax.shift_right_arithmetic(ids[...], 7), (8, LANES)).astype(F32)
@@ -226,34 +224,23 @@
     tile = jnp.concatenate([load, table], axis=0).astype(BF16)
     for p in range(N_SUB):
         msg[p] = tile
-    for move in moves:
-        move.wait()
-
-
-def k_load(recv, oh_hbm, msg, oh, sems):
-    waits = started([(oh_hbm.at[i], oh.at[i]) for i in range(OH_PARTS)], sems)
-    load = jnp.zeros((LOADS, ROWS), F32)
-    for i, wait in enumerate(waits):
-        terms = jnp.concatenate([recv[4 * i + g] for g in range(4)], axis=1)
-        wait.wait()
-        load += nt(terms, oh[i])
-    load = load.astype(BF16)
-    for p in range(N_SUB):
-        msg[p] = load
-
-
-def k_pick_table(recv, where, oh_out, oh_buf, sems):
+
+
+def k_pick_table(recv, where, oh_out, ids_out, oh_buf, sems):
     moves = []
+    slab = []
     base = where[0, 1] * CORNERS
     dof = jnp.concatenate(
         [iota((CORNERS, LANES), 0) + (base + ROWS * g) for g in range(N_GRP)], axis=0
     )
     for p in range(N_SUB):
         row = id_row(recv[p, LOADS : LOADS + 8, :LANES])
+        slab.append(row[:, :OWN])
         oh_buf[p // 4, :, LANES * (p % 4) : LANES * (p % 4 + 1)] = onehot(dof == row)
         if p % 4 == 3:
             moves.append(pltpu.make_async_copy(oh_buf.at[p // 4], oh_out.at[p // 4], sems.at[p // 4]))
             moves[-1].start()
+    ids_out[...] = jnp.concatenate(slab, axis=1)
     for move in moves:
         move.wait()
 
@@ -280,23 +267,6 @@
     values = joined(nt(halves(slab_load(recv)), block[...])).astype(BF16)
     for g in range(N_GRP):
         msg[g] = values
-
-
-def k_solve_last(recv, block, gram, field, local, where, msg):
-    load = slab_load(recv)
-    values = joined(nt(halves(load), block[...])).astype(BF16)
-    energy = dot_rows(field[...], joined(local))
-    lane = iota((LOADS, LANES), 1)
-    sums = roll(spread(jnp.where(lane == 4, energy, gram[...])), CORNERS)
-    chunk = jnp.zeros((LOADS, LANES), F32)
-    for s in range(N_SUB):
-        piece = load[:, CORNERS * s : CORNERS * (s + 1)]
-        piece = jnp.concatenate([piece, jnp.zeros((LOADS, LANES - CORNERS), F32)], axis=1)
-        chunk = jnp.where(where[0, 1] == s, piece, chunk)
-    sums = jnp.where(lane < CORNERS, chunk, sums)
-    tile = jnp.concatenate([values, sums.astype(BF16)], axis=1)
-    for g in range(N_GRP):
-        msg[g] = tile
 
 
 def coarse_sum(recv, start, size):
@@ -320,22 +290,43 @@
             msg[4 * i + p] = picked[:, LANES * p : LANES * (p + 1)]
 
 
-def k_pick_last(recv, oh_hbm, msg, oh, sems):
+def k_chunk(recv, oh_hbm, msg, oh, sems):
     waits = pick_starts(oh_hbm, oh, sems)
-    values = coarse_sum(recv, 0, COLS)
+    load = jnp.zeros((LOADS, COLS), F32)
+    for i, wait in enumerate(waits):
+        terms = jnp.concatenate([recv[4 * i + p] for p in range(4)], axis=1)
+        wait.wait()
+        load += nt(terms, oh[i])
+    load = load.astype(BF16)
+    for g in range(N_GRP):
+        msg[g] = load
+
+
+def corner_tiles(recv, rows):
+    values = joined(nn(halves(coarse_sum(recv, 0, COLS)), rows[...]))
+    pad = jnp.zeros((LOADS, LANES - OWN), F32)
+    return [
+        jnp.concatenate([values[:, OWN * p : OWN * (p + 1)], pad], axis=1) for p in range(N_SUB)
+    ]
+
+
+def k_corner(recv, rows, msg):
+    for p, tile in enumerate(corner_tiles(recv, rows)):
+        msg[p] = tile.astype(BF16)
+
+
+def k_corner_last(recv, rows, terms, gram, field, local, msg):
+    tiles = corner_tiles(recv, rows)
+    energy = jnp.zeros((LOADS, LANES), F32)
+    for p, tile in enumerate(tiles):
+        energy += terms[p].astype(F32) * tile
+    energy = jnp.sum(energy, axis=1, keepdims=True)
+    own = dot_rows(field[...], joined(local))
     lane = iota((LOADS, LANES), 1)
-    sums = jnp.where(lane < CORNERS, 0.0, coarse_sum(recv, COLS, LANES))
-    sums = gathered(roll(sums, LANES - CORNERS))
-    load = [recv[g, :, COLS : COLS + CORNERS].astype(F32) for g in range(N_GRP)]
-    energy = dot_rows(jnp.concatenate(load, axis=1), values)
-    sums = jnp.where(lane == 5, energy, jnp.where(lane < 5, sums, 0.0))
+    sums = jnp.where(lane == 4, own, jnp.where(lane == 5, energy, gram[...]))
     sums = roll(spread(sums), OWN)
-    values = values.astype(BF16)
-    for i, wait in enumerate(waits):
-        wait.wait()
-        picked = nn(values, oh[i])
-        for p in range(4):
-            msg[4 * i + p] = (picked[:, LANES * p : LANES * (p + 1)] + sums).astype(BF16)
+    for p, tile in enumerate(tiles):
+        msg[p] = (tile + sums).astype(BF16)
 
 
 def corner_sum(recv):
@@ -346,7 +337,7 @@
 
 
 def k_correct(recv, chat, local, y_out, peers, below, above):
-    y = joined(local) + nn(corner_sum(recv).astype(BF16), chat[...])
+    y = joined(local) + joined(nn(halves(corner_sum(recv)), chat[...]))
     y_out[...] = y
     pack(y, peers, below, above)
 
@@ -354,11 +345,13 @@
 def k_correct_last(recv, chat, local, y_out, peers, below, above, sums_out):
     total = corner_sum(recv)
     lane = iota((LOADS, LANES), 1)
-    at_corners = jnp.where(lane < OWN, total, 0.0).astype(BF16)
-    y = joined(local) + nn(at_corners, chat[...])
+    y = joined(local) + joined(nn(halves(jnp.where(lane < OWN, total, 0.0)), chat[...]))
     y_out[...] = y
     pack(y, peers, below, above)
-    sums_out[...] = gathered(roll(jnp.where(lane < OWN, 0.0, total), LANES - OWN))
+    sums = gathered(roll(jnp.where(lane < OWN, 0.0, total), LANES - OWN))
+    tile = spread(jnp.where(lane < 6, sums, 0.0)).astype(BF16)
+    for g in range(N_GRP):
+        sums_out[g] = tile
 
 
 def k_smooth(y, peers, lo, hi, counts, schur_hbm, r_out, m_out, peers_out, below, above, schur, sems):
@@ -382,8 +375,8 @@
     b = halves(x)
     b_out[...] = b
     terms = joined(nt(b, chat[...])).astype(BF16)
-    for g in range(N_GRP):
-        msg[g] = terms
+    for p in range(N_SUB):
+        msg[p] = terms
 
 
 def k_search_last(m, peers, lo, hi, counts, chat, r0, p0, q0, x_out, b_out, gram_out, msg):
@@ -392,8 +385,8 @@
     b = halves(w)
     b_out[...] = b
     terms = joined(nt(b, chat[...])).astype(BF16)
-    for g in range(N_GRP):
-        msg[g] = terms
+    for p in range(N_SUB):
+        msg[p] = terms
     r, p, q = r0[...], p0[...], q0[...]
     lane = iota((LOADS, LANES), 1)
     gram = jnp.zeros((LOADS, LANES), F32)
@@ -408,6 +401,7 @@
     rows = [slice(SLAB * i, SLAB * (i + 1)) for i in range(FIELD_PARTS)]
     waits = started([(u_hbm.at[part, :], u.at[part, :]) for part in rows], sems)
     z = jump(y, peers, lo, hi, counts, 1.0)
+    sums = gathered(coarse_sum(sums, 0, LANES))
     rp, pq, rw, qw, local, coarse = (sums[:, i : i + 1] for i in range(6))
     p, q, w = p0[...], q0[...], w0[...]
     first = rp / pq
@@ -417,12 +411,12 @@
     second = inner / curvature
     mult = first * p + second * (grow * p - first * w)
     res = r0[...] - first * q - second * (grow * q - first * z)
-    stacked = jnp.concatenate(list(split3(mult)) + list(split3(res)), axis=0)
+    stacked = jnp.concatenate([halves(mult), halves(res)], axis=0)
     for part, wait in zip(rows, waits):
         wait.wait()
         placed = nt(stacked, u[part, :])
-        mult_out[:, part] = placed[0:16] + placed[16:32] + placed[32:48]
-        res_out[:, part] = placed[48:64] + placed[64:80] + placed[80:96]
+        mult_out[:, part] = placed[0:16] + placed[16:32]
+        res_out[:, part] = placed[32:48] + placed[48:64]
 
 
 def k_columns(rows, out):
@@ -430,16 +424,19 @@
         out[g] = rows[:, ROWS * g : ROWS * (g + 1)]
 
 
-def k_permute(u, blocks, out):
+def k_permute(u, blocks, out, total):
     columns = pl.ds(pl.multiple_of(pl.program_id(0) * IFACE, IFACE), IFACE)
-    total = jnp.zeros((IFACE, LENGTH), F32)
-    for a in range(SUBS):
-        rows = slice(IFACE * a, IFACE * (a + 1))
+    total[...] = jnp.zeros_like(total)
+
+    @pl.loop(0, SUBS)
+    def _(a):
+        rows = pl.ds(pl.multiple_of(a * IFACE, IFACE), IFACE)
         half = lax.dot_general(
             u[rows, columns], blocks[a], (((0,), (0,)), ((), ())), preferred_element_type=F32
         )
-        total += nn(half.astype(BF16), u[rows, :])
-    out[...] = total.astype(BF16)
+        total[...] += nn(half.astype(BF16), u[rows, :])
+
+    out[...] = total[...].astype(BF16)
 
 
 def permuted(u, blocks):
@@ -452,22 +449,75 @@
             pl.BlockSpec((SUBS, IFACE, IFACE), lambda i: (0, 0, 0)),
         ],
         out_specs=pl.BlockSpec((IFACE, LENGTH), lambda i: (i, 0)),
+        scratch_shapes=[pltpu.VMEM((IFACE, LENGTH), F32)],
         compiler_params=pltpu.CompilerParams(vmem_limit_bytes=VMEM_LIMIT),
         name="k_permute",
     )(u, blocks)
 
 
+def k_select(first, rows, ids, *refs):
+    out, total, oh = refs[-3:]
+    i = pl.program_id(0)
+
+    @pl.when(i == 0)
+    def _():
+        total[...] = refs[0][...].astype(F32) if len(refs) == 4 else jnp.zeros_like(total)
+
+    base = (first[0] + i) * IFACE
+
+    @pl.loop(0, IFACE // LANES)
+    def _(j):
+        part = pl.ds(pl.multiple_of(j * LANES, LANES), LANES)
+        oh[part, :] = onehot(iota((LANES, N_SUB * OWN), 0) + (base + j * LANES) == ids[...])
+
+    @pl.loop(0, COLS // SLAB)
+    def _(j):
+        part = pl.ds(pl.multiple_of(j * SLAB, SLAB), SLAB)
+        total[part, :] += nn(rows[part, :], oh[...])
+
+    @pl.when(i == pl.num_programs(0) - 1)
+    def _():
+        out[...] = total[...].astype(BF16)
+
+
+def selected(rows, ids):
+    steps = COARSE // IFACE // SELECTS
+    shape = (COLS, N_SUB * OWN)
+    whole = pl.BlockSpec(shape, lambda i, first: (0, 0))
+    table = ()
+    for n in range(SELECTS):
+        spec = pltpu.PrefetchScalarGridSpec(
+            num_scalar_prefetch=1,
+            grid=(steps,),
+            in_specs=[
+                pl.BlockSpec((COLS, IFACE), lambda i, first: (0, first[0] + i)),
+                pl.BlockSpec((1, N_SUB * OWN), lambda i, first: (0, 0)),
+            ]
+            + [whole for _ in table],
+            out_specs=whole,
+            scratch_shapes=[pltpu.VMEM(shape, F32), pltpu.VMEM((IFACE, shape[1]), BF16)],
+        )
+        held = [pltpu.with_memory_space_constraint(t, pltpu.HBM) for t in table]
+        out = pl.pallas_call(
+            k_select,
+            grid_spec=spec,
+            out_shape=pltpu.HBM(shape, BF16),
+            compiler_params=pltpu.CompilerParams(vmem_limit_bytes=VMEM_LIMIT),
+            name="k_select",
+        )(jnp.full((1,), n * steps, jnp.int32), rows, ids, *held)
+        table = (out,)
+    return table[0]
+
+
 FIELD = ((LOADS, LENGTH), F32)
 FIELD_B = ((LOADS, LENGTH), BF16)
 FIELD_H = ((2 * LOADS, LENGTH), BF16)
-OH_LOAD = ((OH_PARTS, ROWS, 4 * LANES), BF16)
 OH_PICK = ((PICK_PARTS, COLS, 4 * LANES), BF16)
 SQUARE = ((LENGTH, LENGTH), BF16)
 PEERS = ((N_SUB, 8, LANES), F32)
 SIDE = ((LOADS, SLAB), F32)
 TILE = ((LOADS, LANES), F32)
-MSG_TERMS = ((N_GRP, LOADS, LANES), BF16)
-MSG_LOAD = ((N_SUB, LOADS, ROWS), BF16)
+MSG_TERMS = ((N_SUB, LOADS, LANES), BF16)
 MSG_VALUES = ((N_GRP, LOADS, COLS), BF16)
 MSG_CORNERS = ((N_SUB, LOADS, LANES), BF16)
 
@@ -503,9 +553,9 @@
     ids = jnp.pad(corner_ids.reshape(1, OWN), ((0, 0), (0, LANES - OWN)), constant_values=-1)
     where = jnp.stack([lax.axis_index("grp"), lax.axis_index("sub")]).astype(jnp.int32).reshape(1, 2)
 
+    gathered_rows = lax.all_gather(coarse_inverse, "grp", axis=0, tiled=True)
     (block,) = call(k_columns, (((N_GRP, CORNERS, ROWS), BF16),), coarse_inverse)
-    block = over("grp", block)
-    block = block.reshape(COLS, ROWS)
+    block = over("grp", block).reshape(COLS, ROWS)
 
     u, chat, x, msg = call(
         k_setup,
@@ -560,20 +610,13 @@
 
     got = over("grp", msg)
     local = local_of(x)
-    oh_load, msg = call(
-        k_load_first,
-        (OH_LOAD, ((N_SUB, LOADS + 8, ROWS), BF16)),
-        got,
-        ids,
-        where,
-        smem=(2,),
-        out_hbm=(0,),
-        scratch=buffers(OH_LOAD, OH_PARTS),
+    (msg,) = call(
+        k_load_first, (((N_SUB, LOADS + 8, ROWS), BF16),), got, ids, where, smem=(2,)
     )
     got = over("sub", msg)
-    (oh_pick,) = call(
+    oh_pick, slab_ids = call(
         k_pick_table,
-        (OH_PICK,),
+        (OH_PICK, ((1, N_SUB * OWN), jnp.int32)),
         got,
         where,
         smem=(1,),
@@ -590,19 +633,19 @@
     got = exchange(*parts)
     r0, m, *parts = smooth(y, got)
     got = exchange(*parts)
+    table = selected(gathered_rows, slab_ids)
+
+    def chunk(got):
+        (msg,) = call(
+            k_chunk, (MSG_VALUES,), got, oh_pick, hbm=(1,), scratch=buffers(OH_PICK, PICK_PARTS)
+        )
+        return over("grp", msg)
 
     p0, b, msg = call(k_search, (FIELD, FIELD_H, MSG_TERMS), m, *got, counts, chat, smem=(4,))
-    got = over("grp", msg)
+    got = over("sub", msg)
     local = local_of(b)
-    (msg,) = call(
-        k_load, (MSG_LOAD,), got, oh_load, hbm=(1,), scratch=buffers(OH_LOAD, OH_PARTS)
-    )
-    got = over("sub", msg)
-    (msg,) = call(k_solve, (MSG_VALUES,), got, block)
-    got = over("grp", msg)
-    (msg,) = call(
-        k_pick, (MSG_CORNERS,), got, oh_pick, hbm=(1,), scratch=buffers(OH_PICK, PICK_PARTS)
-    )
+    got = chunk(got)
+    (msg,) = call(k_corner, (MSG_CORNERS,), got, table)
     got = over("sub", msg)
     y, *parts = call(k_correct, (FIELD, PEERS, SIDE, SIDE), got, chat, local)
     got = exchange(*parts)
@@ -621,21 +664,20 @@
         q0,
         smem=(4,),
     )
-    got = over("grp", msg)
+    terms = over("sub", msg)
     local = local_of(b)
-    (msg,) = call(
-        k_load, (MSG_LOAD,), got, oh_load, hbm=(1,), scratch=buffers(OH_LOAD, OH_PARTS)
-    )
+    got = chunk(terms)
+    (msg,) = call(k_corner_last, (MSG_CORNERS,), got, table, terms, gram, w0, local)
     got = over("sub", msg)
-    wide = ((N_GRP, LOADS, COLS + LANES), BF16)
-    (msg,) = call(k_solve_last, (wide,), got, block, gram, w0, local, where, smem=(5,))
-    got = over("grp", msg)
-    (msg,) = call(
-        k_pick_last, (MSG_CORNERS,), got, oh_pick, hbm=(1,), scratch=buffers(OH_PICK, PICK_PARTS)
-    )
-    got = over("sub", msg)
-    y, *parts, sums = call(k_correct_last, (FIELD, PEERS, SIDE, SIDE, TILE), got, chat, local)
+    y, *parts, sums = call(
+        k_correct_last,
+        (FIELD, PEERS, SIDE, SIDE, ((N_GRP, LOADS, LANES), BF16)),
+        got,
+        chat,
+        local,
+    )
     got = exchange(*parts)
+    sums = over("grp", sums)
     mult, res = call(
         k_finish,
         (FIELD, FIELD),

time: 405 us -> 449 us (1.11)
  Pallas kernels: 73.6 us -> 129 us
  blocking collectives: 142 us -> 90.8 us
  between operations: 1.18 us -> 14.5 us
  waiting for transfers between devices: 66.2 us -> 78.8 us
  starting transfers between devices: 106 us -> 118 us
    pallas_call x0 -> x4, Pallas kernels: none -> 55.7 us  [selected(): pl.pallas_call(k_select, grid_spec=spec, out_shape=pltpu.HBM(shape, BF16)...]
    all_to_all x7 -> x5, blocking collectives: 142 us -> 90.8 us  [over(): return lax.all_to_all(x, axis, split_axis=0, concat_axis=0, tiled=True)]
    all_to_all x11 -> x12, waiting for transfers between devices: 52.8 us -> 64.6 us  [over(): return lax.all_to_all(x, axis, split_axis=0, concat_axis=0, tiled=True)]
    all_to_all x11 -> x12, starting transfers between devices: 77.2 us -> 88.5 us  [over(): return lax.all_to_all(x, axis, split_axis=0, concat_axis=0, tiled=True)]
    pallas_call x2, Pallas kernels: 27.8 us -> 32.4 us  [permuted(): pl.pallas_call(k_permute, grid=(SUBS,), out_shape=jax.ShapeDtypeStruct((L...]
    pallas_call x20 -> x18, Pallas kernels: 45.8 us -> 41.3 us  [call(): pl.pallas_call(body, out_shape=[pltpu.HBM(s, d) if i in out_hbm else jax....]
  transfers between devices with their start and end apart: 21 -> 23, of which waited for: 13 -> 14; matrix products, arithmetic and copies ran while one was open for 2% -> 2% of each run, Pallas kernels for 8% -> 25%
where the time goes in v1:
time: 449 us; the launch traced here: 447 us
  Pallas kernels  129 us (29%)
  starting transfers between devices  118 us (26%)
  blocking collectives  90.8 us (20%)
  waiting for transfers between devices  78.8 us (18%)
  between operations  14.5 us (3%)
  matrix products  9.58 us (2%)
  local copies, waits for them, and re-layouts  5.74 us (1%)
    all_to_all x5, blocking collectives, over(): return lax.all_to_all(x, axis, split_axis=0, concat_axis=0, tiled=True)  90.8 us
    all_to_all x12, starting transfers between devices, over(): return lax.all_to_all(x, axis, split_axis=0, concat_axis=0, tiled=True)  88.5 us
    all_to_all x12, waiting for transfers between devices, over(): return lax.all_to_all(x, axis, split_axis=0, concat_axis=0, tiled=True)  64.6 us
    pallas_call x4, Pallas kernels, selected(): pl.pallas_call(k_select, grid_spec=spec, out_shape=pltpu.HBM(shape, BF16)...  55.7 us
    pallas_call x18, Pallas kernels, call(): pl.pallas_call(body, out_shape=[pltpu.HBM(s, d) if i in out_hbm else jax....  41.3 us
    pallas_call x2, Pallas kernels, permuted(): pl.pallas_call(k_permute, grid=(SUBS,), out_shape=jax.ShapeDtypeStruct((L...  32.4 us
    ppermute x5, starting transfers between devices, exchange(): up = lax.ppermute(above, 'grp', [(i, i + 1) for i in range(N_GRP - 1)])  19.5 us
    ppermute x5, waiting for transfers between devices, exchange(): down = lax.ppermute(below, 'grp', [(i + 1, i) for i in range(N_GRP - 1)])  13.5 us
  transfers between devices with their start and end apart: 23, of which 14 were waited for; matrix products, arithmetic and copies ran while one was open for 2% of the time, Pallas kernels for 25%

profile of v1, /device:TPU:1, one launch (start us, length us, event | category | flops | bytes accessed | tf_op | source)
XLA Modules:
  0.0 447.4 jit_solution(7711645858867526154)
XLA Ops:
  9.4 6.5 %shard_map.122 = (bf16[1536,1536]{1,0:T(8,128)(2,1)}, bf16[128,1536]{1,0:T(8,128)(2,1)S(1)}, bf16[16,1536]{1,0:T(8,128)(2,1)S(1)}, bf16[32,24,128]{2,1,0:T(8,128)(2,1)}) custom-call(f32[16,6144]{1,0:T(8,128)} %bv_hbm.1, s32[1,384]{1,0:T(1,128)} %bitcast.34, bf16[3,512,128]{2,1,0:T(8,128)(2,1)} %bitcast.30, bf16[16,1536]{1,0:T(8,128)(2,1)} %bitcast.32, ...), custom_call_target="tpu_custom_call" | custom-call | tf_op jit(solution)/shard_map/pallas_call | solution.py:66
  15.9 10.4 %all-to-all-start = ((bf16[32,24,128]{2,1,0:T(8,128)(2,1)}), bf16[32,24,128]{2,1,0:T(8,128)(2,1)S(1)}, u32[]{:S(2)}, u32[]{:S(2)}) async-start(bf16[32,24,128]{2,1,0:T(8,128)(2,1)} %get-tuple-element.40), calls=%async_computation | async-start | bytes 393216 | tf_op jit(solution)/shard_map/all_to_all | solution.py:530
  26.3 1.1 copy-done.3
  28.2 6.4 %all-to-all-done.recv = bf16[32,24,128]{2,1,0:T(8,128)(2,1)S(1)} async-done(((bf16[32,24,128]{2,1,0:T(8,128)(2,1)}), bf16[32,24,128]{2,1,0:T(8,128)(2,1)S(1)}, u32[]{:S(2)}, u32[]{:S(2)}) %all-to-all-start) | async-done | bytes 196640 | tf_op jit(solution)/shard_map/all_to_all | solution.py:530
  34.6 3.8 all-to-all-start.2
  38.5 1.5 shard_map.123
  40.0 15.3 %all-to-all-done.2 = bf16[32,24,384]{2,1,0:T(8,128)(2,1)S(1)} async-done(((bf16[32,24,384]{2,1,0:T(8,128)(2,1)}), bf16[32,24,384]{2,1,0:T(8,128)(2,1)S(1)}, u32[]{:S(2)}, u32[]{:S(2)}) %all-to-all-start.2) | async-done | bytes 589856 | tf_op jit(solution)/shard_map/all_to_all | solution.py:530
  55.3 24.9 %all_to_all.85.recv = bf16[16,24,384]{2,1,0:T(8,128)(2,1)S(1)} all-to-all(bf16[16,24,384]{2,1,0:T(8,128)(2,1)S(1)} %shard_map.123), channel_id=1, replica_groups=mesh['grp'=32,'sub'=16] {'sub'}, dimensions={0} | all-to-all | bytes 589824 | tf_op jit(solution)/shard_map/all_to_all | solution.py:530
  80.2 1.2 shard_map.125
  81.5 13.1 %all-to-all-start.3 = ((bf16[32,16,768]{2,1,0:T(8,128)(2,1)}), bf16[32,16,768]{2,1,0:T(8,128)(2,1)S(1)}, u32[]{:S(2)}, u32[]{:S(2)}) async-start(bf16[32,16,768]{2,1,0:T(8,128)(2,1)} %shard_map.125), calls=%async_computation.3 | async-start | bytes 1572864 | tf_op jit(solution)/shard_map/all_to_all | solution.py:530
  94.6 16.2 %k_permute.2 = bf16[1536,1536]{1,0:T(8,128)(2,1)} custom-call(bf16[1536,1536]{1,0:T(8,128)(2,1)} %get-tuple-element.44.u.u_hbm, bf16[3,512,512]{2,1,0:T(8,128)(2,1)S(1)} %bitcast.22), custom_call_target="tpu_custom_call" | custom-call | tf_op jit(solution)/shard_map/k_permute/pallas_call | solution.py:443
  110.7 2.5 shard_map.126
  113.2 2.5 all-to-all-done.3.recv
  115.7 2.8 shard_map.127
  118.6 5.3 %all-to-all-start.4 = ((bf16[16,16,128]{2,1,0:T(8,128)(2,1)}), bf16[16,16,128]{2,1,0:T(8,128)(2,1)S(1)}, u32[]{:S(2)}, u32[]{:S(2)}) async-start(bf16[16,16,128]{2,1,0:T(8,128)(2,1)} %shard_map.127), calls=%async_computation.4 | async-start | bytes 131072 | tf_op jit(solution)/shard_map/all_to_all | solution.py:530
  123.9 3.1 fusion.local
  126.9 8.5 %all-to-all-done.4.recv = bf16[16,16,128]{2,1,0:T(8,128)(2,1)S(1)} async-done(((bf16[16,16,128]{2,1,0:T(8,128)(2,1)}), bf16[16,16,128]{2,1,0:T(8,128)(2,1)S(1)}, u32[]{:S(2)}, u32[]{:S(2)}) %all-to-all-start.4) | async-done | bytes 65568 | tf_op jit(solution)/shard_map/all_to_all | solution.py:530
  136.3 3.5 all-to-all-start.5
  139.8 6.0 %collective-permute-start = (f32[16,256]{1,0:T(8,128)S(1)}, f32[16,256]{1,0:T(8,128)S(1)}, u32[]{:S(2)}, u32[]{:S(2)}) collective-permute-start(f32[16,256]{1,0:T(8,128)S(1)} %get-tuple-element.47), channel_id=1, source_target_pairs={{0,16},{16,32},{32,48},{48,64},{64,80},{80,96},{96,112},{112,128},... | collective-permute-start | bytes 49160 | tf_op jit(solution)/shard_map/ppermute | solution.py:534
  145.8 1.9 collective-permute-start.1
  147.8 16.2 %k_permute.3.schur_hbm = bf16[1536,1536]{1,0:T(8,128)(2,1)} custom-call(bf16[1536,1536]{1,0:T(8,128)(2,1)} %get-tuple-element.44.u.u_hbm, bf16[3,512,512]{2,1,0:T(8,128)(2,1)S(1)} %bitcast.23), custom_call_target="tpu_custom_call" | custom-call | tf_op jit(solution)/shard_map/k_permute/pallas_call | solution.py:443
  164.0 3.8 shard_map.129
  167.8 11.7 %all-to-all-start.6 = ((f32[16,8,128]{2,1,0:T(8,128)}), f32[16,8,128]{2,1,0:T(8,128)S(1)}, u32[]{:S(2)}, u32[]{:S(2)}) async-start(f32[16,8,128]{2,1,0:T(8,128)} %get-tuple-element.50), calls=%async_computation.6 | async-start | bytes 131072 | tf_op jit(solution)/shard_map/all_to_all | solution.py:530
  179.5 3.9 collective-permute-start.2
  183.4 1.9 collective-permute-start.3
  185.4 3.4 collective-permute-done.3.hi
  188.8 3.0 all-to-all-done.6.peers
  192.6 20.2 %all_to_all.86.recv = bf16[16,16,128]{2,1,0:T(8,128)(2,1)S(1)} all-to-all(bf16[16,16,128]{2,1,0:T(8,128)(2,1)S(1)} %get-tuple-element.53), channel_id=1, replica_groups=mesh['grp'=32,'sub'=16] {'sub'}, dimensions={0} | all-to-all | bytes 131072 | tf_op jit(solution)/shard_map/all_to_all | solution.py:530
  212.8 3.5 shard_map.131
  216.3 9.6 %all-to-all-start.8 = ((bf16[32,16,768]{2,1,0:T(8,128)(2,1)}), bf16[32,16,768]{2,1,0:T(8,128)(2,1)S(1)}, u32[]{:S(2)}, u32[]{:S(2)}) async-start(bf16[32,16,768]{2,1,0:T(8,128)(2,1)} %shard_map.131), calls=%async_computation.8 | async-start | bytes 1572864 | tf_op jit(solution)/shard_map/all_to_all | solution.py:530
  225.9 13.5 %k_select.4.refs_0_ = bf16[768,1152]{1,0:T(8,128)(2,1)} custom-call(s32[1]{0:T(128)} %constant.18.clone.1.first, bf16[768,12288]{1,0:T(8,128)(2,1)} %all-gather.2.cloned.1.call-done.rows, s32[1,1152]{1,0:T(1,128)S(1)} %get-tuple-element.54.ids), custom_call_target="tpu_custom_call" | custom-call | tf_op jit(solution)/shard_map/k_select/pallas_call | solution.py:501
  239.4 14.1 %k_select.5.refs_0_ = bf16[768,1152]{1,0:T(8,128)(2,1)} custom-call(s32[1]{0:T(128)} %constant.17.clone.1.first, bf16[768,12288]{1,0:T(8,128)(2,1)} %all-gather.2.cloned.1.call-done.rows, s32[1,1152]{1,0:T(1,128)S(1)} %get-tuple-element.54.ids, bf16[768,1152]{1,0:T(8,128)(2,1)} %k_select.4.refs_0_), custom_call_target="tpu_custom_call" | custom-call | tf_op jit(solution)/shard_map/k_select/pallas_call | solution.py:501
  253.5 14.1 %k_select.6.refs_0_ = bf16[768,1152]{1,0:T(8,128)(2,1)} custom-call(s32[1]{0:T(128)} %constant.16.clone.1.first, bf16[768,12288]{1,0:T(8,128)(2,1)} %all-gather.2.cloned.1.call-done.rows, s32[1,1152]{1,0:T(1,128)S(1)} %get-tuple-element.54.ids, bf16[768,1152]{1,0:T(8,128)(2,1)} %k_select.5.refs_0_), custom_call_target="tpu_custom_call" | custom-call | tf_op jit(solution)/shard_map/k_select/pallas_call | solution.py:501
  267.6 14.1 %k_select.7.rows = bf16[768,1152]{1,0:T(8,128)(2,1)} custom-call(s32[1]{0:T(128)} %constant.7.clone.1.first, bf16[768,12288]{1,0:T(8,128)(2,1)} %all-gather.2.cloned.1.call-done.rows, s32[1,1152]{1,0:T(1,128)S(1)} %get-tuple-element.54.ids, bf16[768,1152]{1,0:T(8,128)(2,1)} %k_select.6.refs_0_), custom_call_target="tpu_custom_call" | custom-call | tf_op jit(solution)/shard_map/k_select/pallas_call | solution.py:501
  281.6 1.5 copy-done
  283.1 1.1 shard_map.132
  284.3 3.5 all-to-all-start.9
  287.8 3.2 fusion.1.local
  291.0 8.4 %all-to-all-done.9.recv = bf16[16,16,128]{2,1,0:T(8,128)(2,1)S(1)} async-done(((bf16[16,16,128]{2,1,0:T(8,128)(2,1)}), bf16[16,16,128]{2,1,0:T(8,128)(2,1)S(1)}, u32[]{:S(2)}, u32[]{:S(2)}) %all-to-all-start.9) | async-done | bytes 65568 | tf_op jit(solution)/shard_map/all_to_all | solution.py:530
  300.3 3.8 all-to-all-start.10
  304.1 4.9 %collective-permute-start.4 = (f32[16,256]{1,0:T(8,128)S(1)}, f32[16,256]{1,0:T(8,128)S(1)}, u32[]{:S(2)}, u32[]{:S(2)}) collective-permute-start(f32[16,256]{1,0:T(8,128)S(1)} %get-tuple-element.58), channel_id=1, source_target_pairs={{0,16},{16,32},{32,48},{48,64},{64,80},{80,96},{96,112},{112,128},... | collective-permute-start | bytes 49160 | tf_op jit(solution)/shard_map/ppermute | solution.py:534
  309.0 1.9 collective-permute-start.5
  310.9 3.4 collective-permute-done.5.hi
  314.3 1.4 all-to-all-done.10.peers
  315.8 3.8 shard_map.134
  319.6 9.9 %all-to-all-start.11 = ((f32[16,8,128]{2,1,0:T(8,128)}), f32[16,8,128]{2,1,0:T(8,128)S(1)}, u32[]{:S(2)}, u32[]{:S(2)}) async-start(f32[16,8,128]{2,1,0:T(8,128)} %get-tuple-element.61), calls=%async_computation.11 | async-start | bytes 131072 | tf_op jit(solution)/shard_map/all_to_all | solution.py:530
  329.6 2.2 collective-permute-start.6
  331.8 2.1 collective-permute-start.7
  333.9 3.2 collective-permute-done.7.hi
  337.1 4.4 all-to-all-done.11.peers
  343.0 18.8 %all_to_all.87.recv.terms = bf16[16,16,128]{2,1,0:T(8,128)(2,1)S(1)} all-to-all(bf16[16,16,128]{2,1,0:T(8,128)(2,1)S(1)} %get-tuple-element.67), channel_id=1, replica_groups=mesh['grp'=32,'sub'=16] {'sub'}, dimensions={0} | all-to-all | bytes 131072 | tf_op jit(solution)/shard_map/all_to_all | solution.py:530
  361.8 2.8 shard_map.136
  364.6 0.9 copy-done.2
  365.5 10.4 %all-to-all-start.13 = ((bf16[32,16,768]{2,1,0:T(8,128)(2,1)}), bf16[32,16,768]{2,1,0:T(8,128)(2,1)S(1)}, u32[]{:S(2)}, u32[]{:S(2)}) async-start(bf16[32,16,768]{2,1,0:T(8,128)(2,1)} %copy-done.2), calls=%async_computation.13 | async-start | bytes 1572864 | tf_op jit(solution)/shard_map/all_to_all | solution.py:530
  375.9 3.3 fusion.2.local
  379.2 10.9 %all-to-all-done.13.recv = bf16[32,16,768]{2,1,0:T(8,128)(2,1)S(1)} async-done(((bf16[32,16,768]{2,1,0:T(8,128)(2,1)}), bf16[32,16,768]{2,1,0:T(8,128)(2,1)S(1)}, u32[]{:S(2)}, u32[]{:S(2)}) %all-to-all-start.13) | async-done | bytes 786464 | tf_op jit(solution)/shard_map/all_to_all | solution.py:530
  390.9 14.3 %all_to_all.88.recv = bf16[16,16,128]{2,1,0:T(8,128)(2,1)S(1)} all-to-all(bf16[16,16,128]{2,1,0:T(8,128)(2,1)S(1)} %shard_map.137), channel_id=1, replica_groups=mesh['grp'=32,'sub'=16] {'sub'}, dimensions={0} | all-to-all | bytes 131072 | tf_op jit(solution)/shard_map/all_to_all | solution.py:530
  406.0 12.6 %all_to_all.89.sums = bf16[32,16,128]{2,1,0:T(8,128)(2,1)S(1)} all-to-all(bf16[32,16,128]{2,1,0:T(8,128)(2,1)S(1)} %get-tuple-element.75), channel_id=1, replica_groups=mesh['grp'=32,'sub'=16] {'grp'}, dimensions={0} | all-to-all | bytes 262144 | tf_op jit(solution)/shard_map/all_to_all | solution.py:530
  418.6 3.5 all-to-all-start.15
  422.1 2.5 collective-permute-start.8
  424.7 1.9 collective-permute-start.9
  426.6 3.4 collective-permute-done.9.hi
  430.0 3.8 all-to-all-done.15.peers
  434.7 5.9 %shard_map.139 = (f32[16,1536]{1,0:T(8,128)}, f32[16,1536]{1,0:T(8,128)}) custom-call(f32[16,1536]{1,0:T(8,128)S(1)} %get-tuple-element.71.y, f32[16,8,128]{2,1,0:T(8,128)S(1)} %all-to-all-done.15.peers, f32[16,256]{1,0:T(8,128)S(1)} %collective-permute-done.8.lo, f32[16,256]{1,0:T(8,128)S(1)} %collective-permute-done.9.hi, s32[1,18]{1,0:T(1,128)S(1)} %bitcast.29, ...), custom_call_target="tpu_custom_call" | custom-call | tf_op jit(solution)/shard_map/pallas_call | solution.py:66
  (41 shorter events, 9.7 us)
Async XLA Ops:
  7.2 87.4 %copy-start.4 = (bf16[1,1,3,512,512]{4,3,2,1,0:T(8,128)(2,1)S(1)}, bf16[1,1,3,512,512]{4,3,2,1,0:T(8,128)(2,1)}, u32[]{:S(2)}) copy-start(bf16[1,1,3,512,512]{4,3,2,1,0:T(8,128)(2,1)} %param.15) | copy-start | bytes 4718596
  7.2 218.7 %all-gather.2.cloned.1.call-start = ((), (), s32[]{:S(2)}) async-start(), calls=%async_computation.17 | async-start | bytes 19464192 | tf_op jit(solution)/shard_map/all_gather | solution.py:556
  8.7 0.7 copy-start.9
  15.9 18.7 %all-to-all-start = ((bf16[32,24,128]{2,1,0:T(8,128)(2,1)}), bf16[32,24,128]{2,1,0:T(8,128)(2,1)S(1)}, u32[]{:S(2)}, u32[]{:S(2)}) async-start(bf16[32,24,128]{2,1,0:T(8,128)(2,1)} %get-tuple-element.40), calls=%async_computation | async-start | bytes 393216 | tf_op jit(solution)/shard_map/all_to_all | solution.py:530
  26.3 1.1 copy-start.3
  34.6 20.7 %all-to-all-start.2 = ((bf16[32,24,384]{2,1,0:T(8,128)(2,1)}), bf16[32,24,384]{2,1,0:T(8,128)(2,1)S(1)}, u32[]{:S(2)}, u32[]{:S(2)}) async-start(bf16[32,24,384]{2,1,0:T(8,128)(2,1)} %shard_map.124), calls=%async_computation.2 | async-start | bytes 1179648 | tf_op jit(solution)/shard_map/all_to_all | solution.py:530
  81.5 34.3 %all-to-all-start.3 = ((bf16[32,16,768]{2,1,0:T(8,128)(2,1)}), bf16[32,16,768]{2,1,0:T(8,128)(2,1)S(1)}, u32[]{:S(2)}, u32[]{:S(2)}) async-start(bf16[32,16,768]{2,1,0:T(8,128)(2,1)} %shard_map.125), calls=%async_computation.3 | async-start | bytes 1572864 | tf_op jit(solution)/shard_map/all_to_all | solution.py:530
  115.7 32.0 %copy-start.5 = (bf16[1,1,3,512,512]{4,3,2,1,0:T(8,128)(2,1)S(1)}, bf16[1,1,3,512,512]{4,3,2,1,0:T(8,128)(2,1)}, u32[]{:S(2)}) copy-start(bf16[1,1,3,512,512]{4,3,2,1,0:T(8,128)(2,1)} %param.16) | copy-start | bytes 4718596
  118.6 16.9 %all-to-all-start.4 = ((bf16[16,16,128]{2,1,0:T(8,128)(2,1)}), bf16[16,16,128]{2,1,0:T(8,128)(2,1)S(1)}, u32[]{:S(2)}, u32[]{:S(2)}) async-start(bf16[16,16,128]{2,1,0:T(8,128)(2,1)} %shard_map.127), calls=%async_computation.4 | async-start | bytes 131072 | tf_op jit(solution)/shard_map/all_to_all | solution.py:530
  136.3 27.6 %all-to-all-start.5 = ((f32[16,8,128]{2,1,0:T(8,128)}), f32[16,8,128]{2,1,0:T(8,128)S(1)}, u32[]{:S(2)}, u32[]{:S(2)}) async-start(f32[16,8,128]{2,1,0:T(8,128)} %get-tuple-element.46), calls=%async_computation.5 | async-start | bytes 131072 | tf_op jit(solution)/shard_map/all_to_all | solution.py:530
  139.8 24.1 %collective-permute-start = (f32[16,256]{1,0:T(8,128)S(1)}, f32[16,256]{1,0:T(8,128)S(1)}, u32[]{:S(2)}, u32[]{:S(2)}) collective-permute-start(f32[16,256]{1,0:T(8,128)S(1)} %get-tuple-element.47), channel_id=1, source_target_pairs={{0,16},{16,32},{32,48},{48,64},{64,80},{80,96},{96,112},{112,128},... | collective-permute-start | bytes 49160 | tf_op jit(solution)/shard_map/ppermute | solution.py:534
  145.8 18.1 %collective-permute-start.1 = (f32[16,256]{1,0:T(8,128)S(1)}, f32[16,256]{1,0:T(8,128)S(1)}, u32[]{:S(2)}, u32[]{:S(2)}) collective-permute-start(f32[16,256]{1,0:T(8,128)S(1)} %get-tuple-element.48), channel_id=1, source_target_pairs={{16,0},{32,16},{48,32},{64,48},{80,64},{96,80},{112,96},{128,112},... | collective-permute-start | bytes 49160 | tf_op jit(solution)/shard_map/ppermute | solution.py:535
  147.8 16.2 %copy-start.10 = (s32[1,1,18]{2,1,0:T(1,128)S(1)}, s32[1,1,18]{2,1,0:T(1,128)}, u32[]{:S(2)}) copy-start(s32[1,1,18]{2,1,0:T(1,128)} %param.20) | copy-start | bytes 220
  167.8 23.9 %all-to-all-start.6 = ((f32[16,8,128]{2,1,0:T(8,128)}), f32[16,8,128]{2,1,0:T(8,128)S(1)}, u32[]{:S(2)}, u32[]{:S(2)}) async-start(f32[16,8,128]{2,1,0:T(8,128)} %get-tuple-element.50), calls=%async_computation.6 | async-start | bytes 131072 | tf_op jit(solution)/shard_map/all_to_all | solution.py:530
  179.5 5.9 %collective-permute-start.2 = (f32[16,256]{1,0:T(8,128)S(1)}, f32[16,256]{1,0:T(8,128)S(1)}, u32[]{:S(2)}, u32[]{:S(2)}) collective-permute-start(f32[16,256]{1,0:T(8,128)S(1)} %get-tuple-element.51), channel_id=1, source_target_pairs={{0,16},{16,32},{32,48},{48,64},{64,80},{80,96},{96,112},{112,128},... | collective-permute-start | bytes 49160 | tf_op jit(solution)/shard_map/ppermute | solution.py:534
  183.4 5.4 %collective-permute-start.3 = (f32[16,256]{1,0:T(8,128)S(1)}, f32[16,256]{1,0:T(8,128)S(1)}, u32[]{:S(2)}, u32[]{:S(2)}) collective-permute-start(f32[16,256]{1,0:T(8,128)S(1)} %get-tuple-element.52), channel_id=1, source_target_pairs={{16,0},{32,16},{48,32},{64,48},{80,64},{96,80},{112,96},{128,112},... | collective-permute-start | bytes 49160 | tf_op jit(solution)/shard_map/ppermute | solution.py:535
  216.3 65.4 %all-to-all-start.8 = ((bf16[32,16,768]{2,1,0:T(8,128)(2,1)}), bf16[32,16,768]{2,1,0:T(8,128)(2,1)S(1)}, u32[]{:S(2)}, u32[]{:S(2)}) async-start(bf16[32,16,768]{2,1,0:T(8,128)(2,1)} %shard_map.131), calls=%async_computation.8 | async-start | bytes 1572864 | tf_op jit(solution)/shard_map/all_to_all | solution.py:530
  281.6 1.5 copy-start
  284.3 15.2 %all-to-all-start.9 = ((bf16[16,16,128]{2,1,0:T(8,128)(2,1)}), bf16[16,16,128]{2,1,0:T(8,128)(2,1)S(1)}, u32[]{:S(2)}, u32[]{:S(2)}) async-start(bf16[16,16,128]{2,1,0:T(8,128)(2,1)} %shard_map.132), calls=%async_computation.9 | async-start | bytes 131072 | tf_op jit(solution)/shard_map/all_to_all | solution.py:530
  300.3 15.5 %all-to-all-start.10 = ((f32[16,8,128]{2,1,0:T(8,128)}), f32[16,8,128]{2,1,0:T(8,128)S(1)}, u32[]{:S(2)}, u32[]{:S(2)}) async-start(f32[16,8,128]{2,1,0:T(8,128)} %get-tuple-element.57), calls=%async_computation.10 | async-start | bytes 131072 | tf_op jit(solution)/shard_map/all_to_all | solution.py:530
  304.1 6.8 %collective-permute-start.4 = (f32[16,256]{1,0:T(8,128)S(1)}, f32[16,256]{1,0:T(8,128)S(1)}, u32[]{:S(2)}, u32[]{:S(2)}) collective-permute-start(f32[16,256]{1,0:T(8,128)S(1)} %get-tuple-element.58), channel_id=1, source_target_pairs={{0,16},{16,32},{32,48},{48,64},{64,80},{80,96},{96,112},{112,128},... | collective-permute-start | bytes 49160 | tf_op jit(solution)/shard_map/ppermute | solution.py:534
  309.0 5.4 %collective-permute-start.5 = (f32[16,256]{1,0:T(8,128)S(1)}, f32[16,256]{1,0:T(8,128)S(1)}, u32[]{:S(2)}, u32[]{:S(2)}) collective-permute-start(f32[16,256]{1,0:T(8,128)S(1)} %get-tuple-element.59), channel_id=1, source_target_pairs={{16,0},{32,16},{48,32},{64,48},{80,64},{96,80},{112,96},{128,112},... | collective-permute-start | bytes 49160 | tf_op jit(solution)/shard_map/ppermute | solution.py:535
  319.6 22.7 %copy-start.6 = (f32[16,1536]{1,0:T(8,128)}, f32[16,1536]{1,0:T(8,128)S(1)}, u32[]{:S(2)}) copy-start(f32[16,1536]{1,0:T(8,128)S(1)} %get-tuple-element.66.q0) | copy-start | bytes 294916
  319.6 21.9 %all-to-all-start.11 = ((f32[16,8,128]{2,1,0:T(8,128)}), f32[16,8,128]{2,1,0:T(8,128)S(1)}, u32[]{:S(2)}, u32[]{:S(2)}) async-start(f32[16,8,128]{2,1,0:T(8,128)} %get-tuple-element.61), calls=%async_computation.11 | async-start | bytes 131072 | tf_op jit(solution)/shard_map/all_to_all | solution.py:530
  329.6 4.3 collective-permute-start.6
  331.8 5.4 %collective-permute-start.7 = (f32[16,256]{1,0:T(8,128)S(1)}, f32[16,256]{1,0:T(8,128)S(1)}, u32[]{:S(2)}, u32[]{:S(2)}) collective-permute-start(f32[16,256]{1,0:T(8,128)S(1)} %get-tuple-element.63), channel_id=1, source_target_pairs={{16,0},{32,16},{48,32},{64,48},{80,64},{96,80},{112,96},{128,112},... | collective-permute-start | bytes 49160 | tf_op jit(solution)/shard_map/ppermute | solution.py:535
  342.3 0.6 copy-start.8
  361.8 28.3 %copy-start.1 = (bf16[768,1152]{1,0:T(8,128)(2,1)S(1)}, bf16[768,1152]{1,0:T(8,128)(2,1)}, u32[]{:S(2)}) copy-start(bf16[768,1152]{1,0:T(8,128)(2,1)} %k_select.7.rows) | copy-start | bytes 5308420
  364.6 0.9 copy-start.2
  365.5 24.7 %all-to-all-start.13 = ((bf16[32,16,768]{2,1,0:T(8,128)(2,1)}), bf16[32,16,768]{2,1,0:T(8,128)(2,1)S(1)}, u32[]{:S(2)}, u32[]{:S(2)}) async-start(bf16[32,16,768]{2,1,0:T(8,128)(2,1)} %copy-done.2), calls=%async_computation.13 | async-start | bytes 1572864 | tf_op jit(solution)/shard_map/all_to_all | solution.py:530
  418.6 15.2 %all-to-all-start.15 = ((f32[16,8,128]{2,1,0:T(8,128)}), f32[16,8,128]{2,1,0:T(8,128)S(1)}, u32[]{:S(2)}, u32[]{:S(2)}) async-start(f32[16,8,128]{2,1,0:T(8,128)} %get-tuple-element.72), calls=%async_computation.15 | async-start | bytes 131072 | tf_op jit(solution)/shard_map/all_to_all | solution.py:530
  422.1 4.5 collective-permute-start.8
  424.7 5.4 %collective-permute-start.9 = (f32[16,256]{1,0:T(8,128)S(1)}, f32[16,256]{1,0:T(8,128)S(1)}, u32[]{:S(2)}, u32[]{:S(2)}) collective-permute-start(f32[16,256]{1,0:T(8,128)S(1)} %get-tuple-element.74), channel_id=1, source_target_pairs={{16,0},{32,16},{48,32},{64,48},{80,64},{96,80},{112,96},{128,112},... | collective-permute-start | bytes 49160 | tf_op jit(solution)/shard_map/ppermute | solution.py:535
  433.8 0.9 copy-start.7
Sparse Core Ops, SparseCore 0:
  11.1 111.8 all-gather.1

commit v2 on v0

--- a/solution.py
+++ b/solution.py
@@ -26,8 +26,8 @@
 F32 = jnp.float32
 BF16 = jnp.bfloat16
 VMEM_LIMIT = 48 * 1024 * 1024
-OH_PARTS = 8
-PICK_PARTS = 4
+LOAD_PARTS = 6
+PICK_PARTS = 3
 FIELD_PARTS = 6
 
 
@@ -151,13 +151,13 @@
 
 
 def k_setup(
-    bv_hbm, dids_hbm, dc_hbm, loads_hbm, slots_hbm, corner_hbm, ids, counts,
+    bv_hbm, dids_hbm, dc_hbm, loads_hbm, slots_hbm, corner_hbm, inverse_hbm, ids, counts,
     u_out, chat_out, x_out, msg,
-    bv, dids, dc, loads, slots, corner, u_buf, sems, out_sems,
+    bv, dids, dc, loads, slots, corner, inverse, u_buf, sems, out_sems,
 ):
     step = 768
-    sources = (slots_hbm, dids_hbm, bv_hbm, corner_hbm, dc_hbm, loads_hbm)
-    waits = started(tuple(zip(sources, (slots, dids, bv, corner, dc, loads))), sems)
+    sources = (slots_hbm, dids_hbm, bv_hbm, corner_hbm, dc_hbm, loads_hbm, inverse_hbm)
+    waits = started(tuple(zip(sources, (slots, dids, bv, corner, dc, loads, inverse))), sems)
     waits[0].wait()
     moves = []
     for a in range(SUBS):
@@ -195,7 +195,8 @@
     table = jnp.where(row == 0, high, jnp.where(row == 1, low, 0.0))
     tile = jnp.concatenate([terms, table], axis=0).astype(BF16)
     for g in range(N_GRP):
-        msg[g] = tile
+        msg[g, :, :ROWS] = inverse[:, ROWS * g : ROWS * (g + 1)]
+        msg[g, :, ROWS:] = tile
     for move in moves:
         move.wait()
 
@@ -205,63 +206,68 @@
     return (tile[0:1] * 128.0 + tile[1:2]).astype(jnp.int32)
 
 
-def k_load_first(recv, ids, where, oh_out, msg, oh_buf, sems):
-    moves = []
+def k_load_first(recv, ids, where, block_out, msg):
     base = where[0, 0] * ROWS
     load = jnp.zeros((LOADS, ROWS), F32)
     for j in range(N_GRP // 2):
-        pair = [recv[2 * j + i] for i in range(2)]
+        pair = [recv[2 * j + i, :, ROWS:] for i in range(2)]
         row = jnp.concatenate([id_row(t[LOADS:]) for t in pair], axis=1)
         oh = onehot(iota((ROWS, 2 * LANES), 0) + base == row)
-        oh_buf[j // 2, :, 2 * LANES * (j % 2) : 2 * LANES * (j % 2 + 1)] = oh
-        if j % 2:
-            moves.append(pltpu.make_async_copy(oh_buf.at[j // 2], oh_out.at[j // 2], sems.at[j // 2]))
-            moves[-1].start()
         load += nt(jnp.concatenate([t[:LOADS] for t in pair], axis=1), oh)
     row = iota((8, LANES), 0)
     high = jnp.broadcast_to(lax.shift_right_arithmetic(ids[...], 7), (8, LANES)).astype(F32)
     low = jnp.broadcast_to(jnp.bitwise_and(ids[...], 127), (8, LANES)).astype(F32)
     table = jnp.where(row == 0, high, jnp.where(row == 1, low, 0.0))
-    table = jnp.concatenate([table, jnp.zeros((8, ROWS - LANES), F32)], axis=1)
-    tile = jnp.concatenate([load, table], axis=0).astype(BF16)
+    parts = [load[:, LANES * i : LANES * (i + 1)] for i in range(ROWS // LANES)]
+    tile = jnp.concatenate(parts + [table], axis=0).astype(BF16)
     for p in range(N_SUB):
         msg[p] = tile
+    for g in range(N_GRP):
+        block_out[CORNERS * g : CORNERS * (g + 1), :] = recv[g, :, :ROWS]
+
+
+def write_table(dofs, row, out, buf, sems):
+    moves = []
+    for i in range(buf.shape[0]):
+        buf[i] = onehot(dofs == row[:, ROWS * i : ROWS * (i + 1)])
+        moves.append(pltpu.make_async_copy(buf.at[i], out.at[i], sems.at[i]))
+        moves[-1].start()
     for move in moves:
         move.wait()
 
 
+def k_load_table(recv, where, oh_out, oh_buf, sems):
+    rows = [id_row(recv[g, LOADS:, ROWS:])[:, :OWN] for g in range(N_GRP)]
+    dofs = iota((ROWS, ROWS), 0) + where[0, 0] * ROWS
+    write_table(dofs, jnp.concatenate(rows, axis=1), oh_out, oh_buf, sems)
+
+
 def k_load(recv, oh_hbm, msg, oh, sems):
-    waits = started([(oh_hbm.at[i], oh.at[i]) for i in range(OH_PARTS)], sems)
+    waits = started([(oh_hbm.at[i], oh.at[i]) for i in range(LOAD_PARTS)], sems)
+    terms = [recv[g].astype(F32)[:, :OWN] for g in range(N_GRP)]
+    terms = jnp.concatenate(terms, axis=1).astype(BF16)
     load = jnp.zeros((LOADS, ROWS), F32)
     for i, wait in enumerate(waits):
-        terms = jnp.concatenate([recv[4 * i + g] for g in range(4)], axis=1)
         wait.wait()
-        load += nt(terms, oh[i])
+        load += nt(terms[:, ROWS * i : ROWS * (i + 1)], oh[i])
     load = load.astype(BF16)
     for p in range(N_SUB):
         msg[p] = load
 
 
 def k_pick_table(recv, where, oh_out, oh_buf, sems):
-    moves = []
     base = where[0, 1] * CORNERS
-    dof = jnp.concatenate(
-        [iota((CORNERS, LANES), 0) + (base + ROWS * g) for g in range(N_GRP)], axis=0
-    )
-    for p in range(N_SUB):
-        row = id_row(recv[p, LOADS : LOADS + 8, :LANES])
-        oh_buf[p // 4, :, LANES * (p % 4) : LANES * (p % 4 + 1)] = onehot(dof == row)
-        if p % 4 == 3:
-            moves.append(pltpu.make_async_copy(oh_buf.at[p // 4], oh_out.at[p // 4], sems.at[p // 4]))
-            moves[-1].start()
-    for move in moves:
-        move.wait()
+    dofs = jnp.concatenate(
+        [iota((CORNERS, ROWS), 0) + (base + ROWS * g) for g in range(N_GRP)], axis=0
+    )
+    rows = [id_row(recv[p, 3 * LOADS :, :])[:, :OWN] for p in range(N_SUB)]
+    write_table(dofs, jnp.concatenate(rows, axis=1), oh_out, oh_buf, sems)
 
 
 def slab_load(recv):
-    total = recv[0, :LOADS, :].astype(F32)
+    total = recv[0].astype(F32)
     for p in range(1, N_SUB):
-        total += recv[p, :LOADS, :].astype(F32)
+        total += recv[p].astype(F32)
     return total
 
 
@@ -274,6 +280,14 @@
     if x.shape[0] == LOADS:
         return x[...]
     return x[:LOADS] + x[LOADS:]
+
+
+def k_solve_first(recv, block, msg):
+    total = slab_load(recv)
+    load = jnp.concatenate([total[LOADS * i : LOADS * (i + 1)] for i in range(ROWS // LANES)], axis=1)
+    values = joined(nt(halves(load), block[...])).astype(BF16)
+    for g in range(N_GRP):
+        msg[g] = values
 
 
 def k_solve(recv, block, msg):
@@ -306,6 +320,18 @@
     return total
 
 
+def corner_tiles(values, waits, oh):
+    parts = []
+    for i, wait in enumerate(waits):
+        wait.wait()
+        parts.append(nn(values, oh[i]))
+    picked = jnp.concatenate(parts, axis=1)
+    pad = jnp.zeros((LOADS, LANES - OWN), F32)
+    return [
+        jnp.concatenate([picked[:, OWN * p : OWN * (p + 1)], pad], axis=1) for p in range(N_SUB)
+    ]
+
+
 def pick_starts(oh_hbm, oh, sems):
     return started([(oh_hbm.at[i], oh.at[i]) for i in range(PICK_PARTS)], sems)
 
@@ -313,11 +339,8 @@
 def k_pick(recv, oh_hbm, msg, oh, sems):
     waits = pick_starts(oh_hbm, oh, sems)
     values = coarse_sum(recv, 0, COLS).astype(BF16)
-    for i, wait in enumerate(waits):
-        wait.wait()
-        picked = nn(values, oh[i]).astype(BF16)
-        for p in range(4):
-            msg[4 * i + p] = picked[:, LANES * p : LANES * (p + 1)]
+    for p, tile in enumerate(corner_tiles(values, waits, oh)):
+        msg[p] = tile.astype(BF16)
 
 
 def k_pick_last(recv, oh_hbm, msg, oh, sems):
@@ -330,12 +353,8 @@
     energy = dot_rows(jnp.concatenate(load, axis=1), values)
     sums = jnp.where(lane == 5, energy, jnp.where(lane < 5, sums, 0.0))
     sums = roll(spread(sums), OWN)
-    values = values.astype(BF16)
-    for i, wait in enumerate(waits):
-        wait.wait()
-        picked = nn(values, oh[i])
-        for p in range(4):
-            msg[4 * i + p] = (picked[:, LANES * p : LANES * (p + 1)] + sums).astype(BF16)
+    for p, tile in enumerate(corner_tiles(values.astype(BF16), waits, oh)):
+        msg[p] = (tile + sums).astype(BF16)
 
 
 def corner_sum(recv):
@@ -417,17 +436,12 @@
     second = inner / curvature
     mult = first * p + second * (grow * p - first * w)
     res = r0[...] - first * q - second * (grow * q - first * z)
-    stacked = jnp.concatenate(list(split3(mult)) + list(split3(res)), axis=0)
+    stacked = jnp.concatenate([halves(mult), halves(res)], axis=0)
     for part, wait in zip(rows, waits):
         wait.wait()
         placed = nt(stacked, u[part, :])
-        mult_out[:, part] = placed[0:16] + placed[16:32] + placed[32:48]
-        res_out[:, part] = placed[48:64] + placed[64:80] + placed[80:96]
-
-
-def k_columns(rows, out):
-    for g in range(N_GRP):
-        out[g] = rows[:, ROWS * g : ROWS * (g + 1)]
+        mult_out[:, part] = placed[0:16] + placed[16:32]
+        res_out[:, part] = placed[32:48] + placed[48:64]
 
 
 def k_permute(u, blocks, out):
@@ -460,8 +474,8 @@
 FIELD = ((LOADS, LENGTH), F32)
 FIELD_B = ((LOADS, LENGTH), BF16)
 FIELD_H = ((2 * LOADS, LENGTH), BF16)
-OH_LOAD = ((OH_PARTS, ROWS, 4 * LANES), BF16)
-OH_PICK = ((PICK_PARTS, COLS, 4 * LANES), BF16)
+OH_LOAD = ((LOAD_PARTS, ROWS, ROWS), BF16)
+OH_PICK = ((PICK_PARTS, COLS, ROWS), BF16)
 SQUARE = ((LENGTH, LENGTH), BF16)
 PEERS = ((N_SUB, 8, LANES), F32)
 SIDE = ((LOADS, SLAB), F32)
@@ -503,17 +517,13 @@
     ids = jnp.pad(corner_ids.reshape(1, OWN), ((0, 0), (0, LANES - OWN)), constant_values=-1)
     where = jnp.stack([lax.axis_index("grp"), lax.axis_index("sub")]).astype(jnp.int32).reshape(1, 2)
 
-    (block,) = call(k_columns, (((N_GRP, CORNERS, ROWS), BF16),), coarse_inverse)
-    block = over("grp", block)
-    block = block.reshape(COLS, ROWS)
-
     u, chat, x, msg = call(
         k_setup,
         (
             ((LENGTH, LENGTH), BF16),
             ((LANES, LENGTH), BF16),
             FIELD_B,
-            ((N_GRP, LOADS + 8, LANES), BF16),
+            ((N_GRP, CORNERS, ROWS + LANES), BF16),
         ),
         boundary_values,
         dirichlet_ids.reshape(1, SUBS * FIXED),
@@ -521,10 +531,11 @@
         loads[0, 0],
         slot_of[0],
         corner_coupling[0, 0],
+        coarse_inverse,
         ids,
         counts,
-        smem=(7,),
-        hbm=(0, 1, 2, 3, 4, 5),
+        smem=(8,),
+        hbm=(0, 1, 2, 3, 4, 5, 6),
         out_hbm=(0,),
         scratch=(
             pltpu.VMEM((LOADS, BOUNDARY), F32),
@@ -533,8 +544,9 @@
             pltpu.VMEM((LOADS, LENGTH), BF16),
             pltpu.VMEM((1, LENGTH), jnp.int32),
             pltpu.VMEM((SUBS, CORNERS, IFACE), BF16),
+            pltpu.VMEM((CORNERS, COARSE), BF16),
             pltpu.VMEM((LENGTH, LENGTH), BF16),
-            pltpu.SemaphoreType.DMA((6,)),
+            pltpu.SemaphoreType.DMA((7,)),
             pltpu.SemaphoreType.DMA((SUBS,)),
         ),
     )
@@ -560,15 +572,22 @@
 
     got = over("grp", msg)
     local = local_of(x)
-    oh_load, msg = call(
+    block, msg = call(
         k_load_first,
-        (OH_LOAD, ((N_SUB, LOADS + 8, ROWS), BF16)),
+        (((COLS, ROWS), BF16), ((N_SUB, 3 * LOADS + 8, LANES), BF16)),
         got,
         ids,
         where,
         smem=(2,),
+    )
+    (oh_load,) = call(
+        k_load_table,
+        (OH_LOAD,),
+        got,
+        where,
+        smem=(1,),
         out_hbm=(0,),
-        scratch=buffers(OH_LOAD, OH_PARTS),
+        scratch=buffers(OH_LOAD, LOAD_PARTS),
     )
     got = over("sub", msg)
     (oh_pick,) = call(
@@ -580,7 +599,7 @@
         out_hbm=(0,),
         scratch=buffers(OH_PICK, PICK_PARTS),
     )
-    (msg,) = call(k_solve, (MSG_VALUES,), got, block)
+    (msg,) = call(k_solve_first, (MSG_VALUES,), got, block)
     got = over("grp", msg)
     (msg,) = call(
         k_pick, (MSG_CORNERS,), got, oh_pick, hbm=(1,), scratch=buffers(OH_PICK, PICK_PARTS)
@@ -595,7 +614,7 @@
     got = over("grp", msg)
     local = local_of(b)
     (msg,) = call(
-        k_load, (MSG_LOAD,), got, oh_load, hbm=(1,), scratch=buffers(OH_LOAD, OH_PARTS)
+        k_load, (MSG_LOAD,), got, oh_load, hbm=(1,), scratch=buffers(OH_LOAD, LOAD_PARTS)
     )
     got = over("sub", msg)
     (msg,) = call(k_solve, (MSG_VALUES,), got, block)
@@ -624,7 +643,7 @@
     got = over("grp", msg)
     local = local_of(b)
     (msg,) = call(
-        k_load, (MSG_LOAD,), got, oh_load, hbm=(1,), scratch=buffers(OH_LOAD, OH_PARTS)
+        k_load, (MSG_LOAD,), got, oh_load, hbm=(1,), scratch=buffers(OH_LOAD, LOAD_PARTS)
     )
     got = over("sub", msg)
     wide = ((N_GRP, LOADS, COLS + LANES), BF16)

time: 405 us -> 395 us (0.975)
  blocking collectives: 142 us -> 125 us
  waiting for transfers between devices: 66.2 us -> 70.6 us
    all_to_all x7 -> x6, blocking collectives: 142 us -> 125 us  [over(): return lax.all_to_all(x, axis, split_axis=0, concat_axis=0, tiled=True)]
    all_to_all x11, waiting for transfers between devices: 52.8 us -> 57.1 us  [over(): return lax.all_to_all(x, axis, split_axis=0, concat_axis=0, tiled=True)]
where the time goes in v2:
time: 395 us; the launch traced here: 392 us
  blocking collectives  125 us (32%)
  starting transfers between devices  110 us (28%)
  Pallas kernels  71.4 us (18%)
  waiting for transfers between devices  70.6 us (18%)
  matrix products  9.52 us (2%)
  local copies, waits for them, and re-layouts  4.04 us (1%)
    all_to_all x6, blocking collectives, over(): return lax.all_to_all(x, axis, split_axis=0, concat_axis=0, tiled=True)  125 us
    all_to_all x11, starting transfers between devices, over(): return lax.all_to_all(x, axis, split_axis=0, concat_axis=0, tiled=True)  80.7 us
    all_to_all x11, waiting for transfers between devices, over(): return lax.all_to_all(x, axis, split_axis=0, concat_axis=0, tiled=True)  57.1 us
    pallas_call x20, Pallas kernels, call(): pl.pallas_call(body, out_shape=[pltpu.HBM(s, d) if i in out_hbm else jax....  43.5 us
    pallas_call x2, Pallas kernels, permuted(): pl.pallas_call(k_permute, grid=(SUBS,), out_shape=jax.ShapeDtypeStruct((L...  27.9 us
    ppermute x5, starting transfers between devices, exchange(): up = lax.ppermute(above, 'grp', [(i, i + 1) for i in range(N_GRP - 1)])  19.1 us
    ppermute x5, waiting for transfers between devices, exchange(): down = lax.ppermute(below, 'grp', [(i + 1, i) for i in range(N_GRP - 1)])  13.5 us
    ppermute x5, starting transfers between devices, exchange(): down = lax.ppermute(below, 'grp', [(i + 1, i) for i in range(N_GRP - 1)])  9.97 us
  transfers between devices with their start and end apart: 21, of which 13 were waited for; matrix products, arithmetic and copies ran while one was open for 2% of the time, Pallas kernels for 8%

profile of v2, /device:TPU:1, one launch (start us, length us, event | category | flops | bytes accessed | tf_op | source)
XLA Modules:
  0.0 392.1 jit_solution(15110895137968074901)
XLA Ops:
  2.1 6.1 %shard_map.122 = (bf16[1536,1536]{1,0:T(8,128)(2,1)}, bf16[128,1536]{1,0:T(8,128)(2,1)S(1)}, bf16[16,1536]{1,0:T(8,128)(2,1)S(1)}, bf16[32,24,512]{2,1,0:T(8,128)(2,1)}) custom-call(f32[16,6144]{1,0:T(8,128)} %bv_hbm.1, s32[1,384]{1,0:T(1,128)} %bitcast.32, bf16[3,512,128]{2,1,0:T(8,128)(2,1)} %bitcast.28, bf16[16,1536]{1,0:T(8,128)(2,1)} %bitcast.30, ...), custom_call_target="tpu_custom_call" | custom-call | tf_op jit(solution)/shard_map/pallas_call | solution.py:66
  8.2 10.4 %all-to-all-start = ((bf16[32,24,512]{2,1,0:T(8,128)(2,1)}), bf16[32,24,512]{2,1,0:T(8,128)(2,1)S(1)}, u32[]{:S(2)}, u32[]{:S(2)}) async-start(bf16[32,24,512]{2,1,0:T(8,128)(2,1)} %get-tuple-element.40), calls=%async_computation | async-start | bytes 1572864 | tf_op jit(solution)/shard_map/all_to_all | solution.py:494
  18.7 14.3 %all-to-all-done.recv = bf16[32,24,512]{2,1,0:T(8,128)(2,1)S(1)} async-done(((bf16[32,24,512]{2,1,0:T(8,128)(2,1)}), bf16[32,24,512]{2,1,0:T(8,128)(2,1)S(1)}, u32[]{:S(2)}, u32[]{:S(2)}) %all-to-all-start) | async-done | bytes 786464 | tf_op jit(solution)/shard_map/all_to_all | solution.py:494
  33.0 1.5 shard_map.123
  34.5 26.0 %all_to_all.85.recv = bf16[16,56,128]{2,1,0:T(8,128)(2,1)S(1)} all-to-all(bf16[16,56,128]{2,1,0:T(8,128)(2,1)S(1)} %get-tuple-element.41), channel_id=1, replica_groups=mesh['grp'=32,'sub'=16] {'sub'}, dimensions={0} | all-to-all | bytes 458752 | tf_op jit(solution)/shard_map/all_to_all | solution.py:494
  60.5 1.2 shard_map.124
  61.7 8.4 %all-to-all-start.2 = ((bf16[32,16,768]{2,1,0:T(8,128)(2,1)}), bf16[32,16,768]{2,1,0:T(8,128)(2,1)S(1)}, u32[]{:S(2)}, u32[]{:S(2)}) async-start(bf16[32,16,768]{2,1,0:T(8,128)(2,1)} %shard_map.124), calls=%async_computation.2 | async-start | bytes 1572864 | tf_op jit(solution)/shard_map/all_to_all | solution.py:494
  70.1 1.4 copy-done
  71.5 13.9 %k_permute.2 = bf16[1536,1536]{1,0:T(8,128)(2,1)} custom-call(bf16[1536,1536]{1,0:T(8,128)(2,1)} %get-tuple-element.45.u.u_hbm, bf16[3,512,512]{2,1,0:T(8,128)(2,1)S(1)} %bitcast.20), custom_call_target="tpu_custom_call" | custom-call | tf_op jit(solution)/shard_map/k_permute/pallas_call | solution.py:460
  85.5 2.0 shard_map.125.oh_hbm
  87.5 2.4 shard_map.126
  90.0 5.6 %all-to-all-start.3 = ((bf16[16,16,128]{2,1,0:T(8,128)(2,1)}), bf16[16,16,128]{2,1,0:T(8,128)(2,1)S(1)}, u32[]{:S(2)}, u32[]{:S(2)}) async-start(bf16[16,16,128]{2,1,0:T(8,128)(2,1)} %shard_map.126), calls=%async_computation.3 | async-start | bytes 131072 | tf_op jit(solution)/shard_map/all_to_all | solution.py:494
  95.6 3.1 fusion.local
  98.7 8.5 %all-to-all-done.3.recv = bf16[16,16,128]{2,1,0:T(8,128)(2,1)S(1)} async-done(((bf16[16,16,128]{2,1,0:T(8,128)(2,1)}), bf16[16,16,128]{2,1,0:T(8,128)(2,1)S(1)}, u32[]{:S(2)}, u32[]{:S(2)}) %all-to-all-start.3) | async-done | bytes 65568 | tf_op jit(solution)/shard_map/all_to_all | solution.py:494
  109.8 4.0 %all-to-all-start.4 = ((f32[16,8,128]{2,1,0:T(8,128)}), f32[16,8,128]{2,1,0:T(8,128)S(1)}, u32[]{:S(2)}, u32[]{:S(2)}) async-start(f32[16,8,128]{2,1,0:T(8,128)} %copy-done.4), calls=%async_computation.4 | async-start | bytes 131072 | tf_op jit(solution)/shard_map/all_to_all | solution.py:494
  113.8 4.9 %collective-permute-start = (f32[16,256]{1,0:T(8,128)}, f32[16,256]{1,0:T(8,128)S(1)}, u32[]{:S(2)}, u32[]{:S(2)}) collective-permute-start(f32[16,256]{1,0:T(8,128)} %get-tuple-element.48), channel_id=1, source_target_pairs={{0,16},{16,32},{32,48},{48,64},{64,80},{80,96},{96,112},{112,128},... | collective-permute-start | bytes 49160 | tf_op jit(solution)/shard_map/ppermute | solution.py:498
  118.7 2.1 collective-permute-start.1
  120.8 13.9 %k_permute.3.schur_hbm = bf16[1536,1536]{1,0:T(8,128)(2,1)} custom-call(bf16[1536,1536]{1,0:T(8,128)(2,1)} %get-tuple-element.45.u.u_hbm, bf16[3,512,512]{2,1,0:T(8,128)(2,1)S(1)} %bitcast.21), custom_call_target="tpu_custom_call" | custom-call | tf_op jit(solution)/shard_map/k_permute/pallas_call | solution.py:460
  134.8 3.8 shard_map.128
  138.6 11.7 %all-to-all-start.5 = ((f32[16,8,128]{2,1,0:T(8,128)}), f32[16,8,128]{2,1,0:T(8,128)S(1)}, u32[]{:S(2)}, u32[]{:S(2)}) async-start(f32[16,8,128]{2,1,0:T(8,128)} %get-tuple-element.51), calls=%async_computation.5 | async-start | bytes 131072 | tf_op jit(solution)/shard_map/all_to_all | solution.py:494
  150.3 3.9 collective-permute-start.2
  154.2 1.9 collective-permute-start.3
  156.2 3.4 collective-permute-done.3.hi
  159.6 2.4 all-to-all-done.5.peers
  161.9 1.5 shard_map.129
  163.4 8.9 %all-to-all-start.6 = ((bf16[32,16,128]{2,1,0:T(8,128)(2,1)}), bf16[32,16,128]{2,1,0:T(8,128)(2,1)S(1)}, u32[]{:S(2)}, u32[]{:S(2)}) async-start(bf16[32,16,128]{2,1,0:T(8,128)(2,1)} %get-tuple-element.54), calls=%async_computation.6 | async-start | bytes 262144 | tf_op jit(solution)/shard_map/all_to_all | solution.py:494
  172.3 2.0 shard_map.130.oh_hbm
  174.2 5.6 %all-to-all-done.6.recv = bf16[32,16,128]{2,1,0:T(8,128)(2,1)S(1)} async-done(((bf16[32,16,128]{2,1,0:T(8,128)(2,1)}), bf16[32,16,128]{2,1,0:T(8,128)(2,1)S(1)}, u32[]{:S(2)}, u32[]{:S(2)}) %all-to-all-start.6) | async-done | bytes 131104 | tf_op jit(solution)/shard_map/all_to_all | solution.py:494
  179.9 1.9 shard_map.131
  181.8 23.2 %all_to_all.86.recv = bf16[16,16,384]{2,1,0:T(8,128)(2,1)S(1)} all-to-all(bf16[16,16,384]{2,1,0:T(8,128)(2,1)S(1)} %shard_map.131), channel_id=1, replica_groups=mesh['grp'=32,'sub'=16] {'sub'}, dimensions={0} | all-to-all | bytes 393216 | tf_op jit(solution)/shard_map/all_to_all | solution.py:494
  205.3 21.5 %all_to_all.87.recv = bf16[32,16,768]{2,1,0:T(8,128)(2,1)S(1)} all-to-all(bf16[32,16,768]{2,1,0:T(8,128)(2,1)S(1)} %shard_map.132), channel_id=1, replica_groups=mesh['grp'=32,'sub'=16] {'grp'}, dimensions={0} | all-to-all | bytes 1572864 | tf_op jit(solution)/shard_map/all_to_all | solution.py:494
  226.9 2.4 shard_map.133
  229.3 5.3 %all-to-all-start.9 = ((bf16[16,16,128]{2,1,0:T(8,128)(2,1)}), bf16[16,16,128]{2,1,0:T(8,128)(2,1)S(1)}, u32[]{:S(2)}, u32[]{:S(2)}) async-start(bf16[16,16,128]{2,1,0:T(8,128)(2,1)} %shard_map.133), calls=%async_computation.9 | async-start | bytes 131072 | tf_op jit(solution)/shard_map/all_to_all | solution.py:494
  234.6 3.2 fusion.1.local
  237.8 8.3 %all-to-all-done.9.recv = bf16[16,16,128]{2,1,0:T(8,128)(2,1)S(1)} async-done(((bf16[16,16,128]{2,1,0:T(8,128)(2,1)}), bf16[16,16,128]{2,1,0:T(8,128)(2,1)S(1)}, u32[]{:S(2)}, u32[]{:S(2)}) %all-to-all-start.9) | async-done | bytes 65568 | tf_op jit(solution)/shard_map/all_to_all | solution.py:494
  246.1 0.9 shard_map.134
  247.0 3.8 all-to-all-start.10
  250.8 4.2 %collective-permute-start.4 = (f32[16,256]{1,0:T(8,128)S(1)}, f32[16,256]{1,0:T(8,128)S(1)}, u32[]{:S(2)}, u32[]{:S(2)}) collective-permute-start(f32[16,256]{1,0:T(8,128)S(1)} %get-tuple-element.58), channel_id=1, source_target_pairs={{0,16},{16,32},{32,48},{48,64},{64,80},{80,96},{96,112},{112,128},... | collective-permute-start | bytes 49160 | tf_op jit(solution)/shard_map/ppermute | solution.py:498
  255.0 1.9 collective-permute-start.5
  256.9 3.4 collective-permute-done.5.hi
  260.4 2.0 all-to-all-done.10.peers
  262.4 3.8 shard_map.135
  266.2 9.3 %all-to-all-start.11 = ((f32[16,8,128]{2,1,0:T(8,128)}), f32[16,8,128]{2,1,0:T(8,128)S(1)}, u32[]{:S(2)}, u32[]{:S(2)}) async-start(f32[16,8,128]{2,1,0:T(8,128)} %get-tuple-element.61), calls=%async_computation.11 | async-start | bytes 131072 | tf_op jit(solution)/shard_map/all_to_all | solution.py:494
  275.6 2.2 collective-permute-start.6
  277.8 2.1 collective-permute-start.7
  279.9 3.2 collective-permute-done.7.hi
  283.1 4.4 %all-to-all-done.11.peers = f32[16,8,128]{2,1,0:T(8,128)S(1)} async-done(((f32[16,8,128]{2,1,0:T(8,128)}), f32[16,8,128]{2,1,0:T(8,128)S(1)}, u32[]{:S(2)}, u32[]{:S(2)}) %all-to-all-start.11) | async-done | bytes 65568 | tf_op jit(solution)/shard_map/all_to_all | solution.py:494
  287.5 0.8 shard_map.136
  288.4 14.4 %all_to_all.88.recv = bf16[32,16,128]{2,1,0:T(8,128)(2,1)S(1)} all-to-all(bf16[32,16,128]{2,1,0:T(8,128)(2,1)S(1)} %get-tuple-element.67), channel_id=1, replica_groups=mesh['grp'=32,'sub'=16] {'grp'}, dimensions={0} | all-to-all | bytes 262144 | tf_op jit(solution)/shard_map/all_to_all | solution.py:494
  302.7 2.6 shard_map.137
  305.3 9.5 %all-to-all-start.13 = ((bf16[16,16,384]{2,1,0:T(8,128)(2,1)}), bf16[16,16,384]{2,1,0:T(8,128)(2,1)S(1)}, u32[]{:S(2)}, u32[]{:S(2)}) async-start(bf16[16,16,384]{2,1,0:T(8,128)(2,1)} %shard_map.137), calls=%async_computation.13 | async-start | bytes 393216 | tf_op jit(solution)/shard_map/all_to_all | solution.py:494
  314.8 3.2 fusion.2.local
  318.0 9.4 %all-to-all-done.13.recv = bf16[16,16,384]{2,1,0:T(8,128)(2,1)S(1)} async-done(((bf16[16,16,384]{2,1,0:T(8,128)(2,1)}), bf16[16,16,384]{2,1,0:T(8,128)(2,1)S(1)}, u32[]{:S(2)}, u32[]{:S(2)}) %all-to-all-start.13) | async-done | bytes 196640 | tf_op jit(solution)/shard_map/all_to_all | solution.py:494
  327.4 0.8 shard_map.138
  328.3 22.9 %all_to_all.89.recv = bf16[32,16,896]{2,1,0:T(8,128)(2,1)S(1)} all-to-all(bf16[32,16,896]{2,1,0:T(8,128)(2,1)S(1)} %shard_map.138), channel_id=1, replica_groups=mesh['grp'=32,'sub'=16] {'grp'}, dimensions={0} | all-to-all | bytes 1835008 | tf_op jit(solution)/shard_map/all_to_all | solution.py:494
  351.2 2.0 shard_map.139
  353.2 16.6 %all_to_all.90.recv = bf16[16,16,128]{2,1,0:T(8,128)(2,1)S(1)} all-to-all(bf16[16,16,128]{2,1,0:T(8,128)(2,1)S(1)} %shard_map.139), channel_id=1, replica_groups=mesh['grp'=32,'sub'=16] {'sub'}, dimensions={0} | all-to-all | bytes 131072 | tf_op jit(solution)/shard_map/all_to_all | solution.py:494
  369.8 0.9 shard_map.140
  370.6 4.0 %all-to-all-start.16 = ((f32[16,8,128]{2,1,0:T(8,128)}), f32[16,8,128]{2,1,0:T(8,128)S(1)}, u32[]{:S(2)}, u32[]{:S(2)}) async-start(f32[16,8,128]{2,1,0:T(8,128)} %get-tuple-element.72), calls=%async_computation.16 | async-start | bytes 131072 | tf_op jit(solution)/shard_map/all_to_all | solution.py:494
  374.6 4.0 %collective-permute-start.8 = (f32[16,256]{1,0:T(8,128)S(1)}, f32[16,256]{1,0:T(8,128)S(1)}, u32[]{:S(2)}, u32[]{:S(2)}) collective-permute-start(f32[16,256]{1,0:T(8,128)S(1)} %get-tuple-element.73), channel_id=1, source_target_pairs={{0,16},{16,32},{32,48},{48,64},{64,80},{80,96},{96,112},{112,128},... | collective-permute-start | bytes 49160 | tf_op jit(solution)/shard_map/ppermute | solution.py:498
  378.6 1.9 collective-permute-start.9
  380.5 3.4 collective-permute-done.9.hi
  383.9 2.2 all-to-all-done.16.peers
  386.2 5.8 %shard_map.141 = (f32[16,1536]{1,0:T(8,128)}, f32[16,1536]{1,0:T(8,128)}) custom-call(f32[16,1536]{1,0:T(8,128)S(1)} %get-tuple-element.71.y, f32[16,8,128]{2,1,0:T(8,128)S(1)} %all-to-all-done.16.peers, f32[16,256]{1,0:T(8,128)S(1)} %collective-permute-done.8.lo, f32[16,256]{1,0:T(8,128)S(1)} %collective-permute-done.9.hi, s32[1,18]{1,0:T(1,128)S(1)} %bitcast.27, ...), custom_call_target="tpu_custom_call" | custom-call | tf_op jit(solution)/shard_map/pallas_call | solution.py:66
  (33 shorter events, 4.5 us)
Async XLA Ops:
  1.4 0.7 copy-start.5
  8.2 24.8 %all-to-all-start = ((bf16[32,24,512]{2,1,0:T(8,128)(2,1)}), bf16[32,24,512]{2,1,0:T(8,128)(2,1)S(1)}, u32[]{:S(2)}, u32[]{:S(2)}) async-start(bf16[32,24,512]{2,1,0:T(8,128)(2,1)} %get-tuple-element.40), calls=%async_computation | async-start | bytes 1572864 | tf_op jit(solution)/shard_map/all_to_all | solution.py:494
  18.7 66.8 %copy-start.7 = (s32[1,2]{1,0:T(1,128)}, s32[1,2]{1,0:T(1,128)S(1)}, u32[]{:S(2)}) copy-start(s32[1,2]{1,0:T(1,128)S(1)} %add_bitcast_fusion.where) | copy-start | bytes 28
  61.7 25.8 %all-to-all-start.2 = ((bf16[32,16,768]{2,1,0:T(8,128)(2,1)}), bf16[32,16,768]{2,1,0:T(8,128)(2,1)S(1)}, u32[]{:S(2)}, u32[]{:S(2)}) async-start(bf16[32,16,768]{2,1,0:T(8,128)(2,1)} %shard_map.124), calls=%async_computation.2 | async-start | bytes 1572864 | tf_op jit(solution)/shard_map/all_to_all | solution.py:494
  70.1 1.4 copy-start
  90.0 30.8 %copy-start.1 = (bf16[1,1,3,512,512]{4,3,2,1,0:T(8,128)(2,1)S(1)}, bf16[1,1,3,512,512]{4,3,2,1,0:T(8,128)(2,1)}, u32[]{:S(2)}) copy-start(bf16[1,1,3,512,512]{4,3,2,1,0:T(8,128)(2,1)} %param.16) | copy-start | bytes 4718596
  90.0 17.2 %all-to-all-start.3 = ((bf16[16,16,128]{2,1,0:T(8,128)(2,1)}), bf16[16,16,128]{2,1,0:T(8,128)(2,1)S(1)}, u32[]{:S(2)}, u32[]{:S(2)}) async-start(bf16[16,16,128]{2,1,0:T(8,128)(2,1)} %shard_map.126), calls=%async_computation.3 | async-start | bytes 131072 | tf_op jit(solution)/shard_map/all_to_all | solution.py:494
  108.0 0.6 copy-start.2
  108.6 0.6 copy-start.4
  109.2 0.6 copy-start.9
  109.8 24.9 %all-to-all-start.4 = ((f32[16,8,128]{2,1,0:T(8,128)}), f32[16,8,128]{2,1,0:T(8,128)S(1)}, u32[]{:S(2)}, u32[]{:S(2)}) async-start(f32[16,8,128]{2,1,0:T(8,128)} %copy-done.4), calls=%async_computation.4 | async-start | bytes 131072 | tf_op jit(solution)/shard_map/all_to_all | solution.py:494
  113.8 20.9 %collective-permute-start = (f32[16,256]{1,0:T(8,128)}, f32[16,256]{1,0:T(8,128)S(1)}, u32[]{:S(2)}, u32[]{:S(2)}) collective-permute-start(f32[16,256]{1,0:T(8,128)} %get-tuple-element.48), channel_id=1, source_target_pairs={{0,16},{16,32},{32,48},{48,64},{64,80},{80,96},{96,112},{112,128},... | collective-permute-start | bytes 49160 | tf_op jit(solution)/shard_map/ppermute | solution.py:498
  118.7 16.1 %collective-permute-start.1 = (f32[16,256]{1,0:T(8,128)}, f32[16,256]{1,0:T(8,128)S(1)}, u32[]{:S(2)}, u32[]{:S(2)}) collective-permute-start(f32[16,256]{1,0:T(8,128)} %copy-done.9), channel_id=1, source_target_pairs={{16,0},{32,16},{48,32},{64,48},{80,64},{96,80},{112,96},{128,112},... | collective-permute-start | bytes 49160 | tf_op jit(solution)/shard_map/ppermute | solution.py:499
  120.8 14.0 %copy-start.3 = (f32[16,1536]{1,0:T(8,128)S(1)}, f32[16,1536]{1,0:T(8,128)}, u32[]{:S(2)}) copy-start(f32[16,1536]{1,0:T(8,128)} %copy-done.2) | copy-start | bytes 294916
  120.8 14.0 %copy-start.6 = (s32[1,1,18]{2,1,0:T(1,128)S(1)}, s32[1,1,18]{2,1,0:T(1,128)}, u32[]{:S(2)}) copy-start(s32[1,1,18]{2,1,0:T(1,128)} %param.20) | copy-start | bytes 220
  134.7 37.5 %copy-start.8 = (s32[1,2]{1,0:T(1,128)S(1)}, s32[1,2]{1,0:T(1,128)}, u32[]{:S(2)}) copy-start(s32[1,2]{1,0:T(1,128)} %copy-done.7) | copy-start | bytes 28
  138.6 23.3 %all-to-all-start.5 = ((f32[16,8,128]{2,1,0:T(8,128)}), f32[16,8,128]{2,1,0:T(8,128)S(1)}, u32[]{:S(2)}, u32[]{:S(2)}) async-start(f32[16,8,128]{2,1,0:T(8,128)} %get-tuple-element.51), calls=%async_computation.5 | async-start | bytes 131072 | tf_op jit(solution)/shard_map/all_to_all | solution.py:494
  150.3 5.8 %collective-permute-start.2 = (f32[16,256]{1,0:T(8,128)S(1)}, f32[16,256]{1,0:T(8,128)S(1)}, u32[]{:S(2)}, u32[]{:S(2)}) collective-permute-start(f32[16,256]{1,0:T(8,128)S(1)} %get-tuple-element.52), channel_id=1, source_target_pairs={{0,16},{16,32},{32,48},{48,64},{64,80},{80,96},{96,112},{112,128},... | collective-permute-start | bytes 49160 | tf_op jit(solution)/shard_map/ppermute | solution.py:498
  154.2 5.4 %collective-permute-start.3 = (f32[16,256]{1,0:T(8,128)S(1)}, f32[16,256]{1,0:T(8,128)S(1)}, u32[]{:S(2)}, u32[]{:S(2)}) collective-permute-start(f32[16,256]{1,0:T(8,128)S(1)} %get-tuple-element.53), channel_id=1, source_target_pairs={{16,0},{32,16},{48,32},{64,48},{80,64},{96,80},{112,96},{128,112},... | collective-permute-start | bytes 49160 | tf_op jit(solution)/shard_map/ppermute | solution.py:499
  163.4 16.5 %all-to-all-start.6 = ((bf16[32,16,128]{2,1,0:T(8,128)(2,1)}), bf16[32,16,128]{2,1,0:T(8,128)(2,1)S(1)}, u32[]{:S(2)}, u32[]{:S(2)}) async-start(bf16[32,16,128]{2,1,0:T(8,128)(2,1)} %get-tuple-element.54), calls=%async_computation.6 | async-start | bytes 262144 | tf_op jit(solution)/shard_map/all_to_all | solution.py:494
  229.3 16.8 %all-to-all-start.9 = ((bf16[16,16,128]{2,1,0:T(8,128)(2,1)}), bf16[16,16,128]{2,1,0:T(8,128)(2,1)S(1)}, u32[]{:S(2)}, u32[]{:S(2)}) async-start(bf16[16,16,128]{2,1,0:T(8,128)(2,1)} %shard_map.133), calls=%async_computation.9 | async-start | bytes 131072 | tf_op jit(solution)/shard_map/all_to_all | solution.py:494
  247.0 15.4 %all-to-all-start.10 = ((f32[16,8,128]{2,1,0:T(8,128)}), f32[16,8,128]{2,1,0:T(8,128)S(1)}, u32[]{:S(2)}, u32[]{:S(2)}) async-start(f32[16,8,128]{2,1,0:T(8,128)} %get-tuple-element.57), calls=%async_computation.10 | async-start | bytes 131072 | tf_op jit(solution)/shard_map/all_to_all | solution.py:494
  250.8 6.1 %collective-permute-start.4 = (f32[16,256]{1,0:T(8,128)S(1)}, f32[16,256]{1,0:T(8,128)S(1)}, u32[]{:S(2)}, u32[]{:S(2)}) collective-permute-start(f32[16,256]{1,0:T(8,128)S(1)} %get-tuple-element.58), channel_id=1, source_target_pairs={{0,16},{16,32},{32,48},{48,64},{64,80},{80,96},{96,112},{112,128},... | collective-permute-start | bytes 49160 | tf_op jit(solution)/shard_map/ppermute | solution.py:498
  255.0 5.4 %collective-permute-start.5 = (f32[16,256]{1,0:T(8,128)S(1)}, f32[16,256]{1,0:T(8,128)S(1)}, u32[]{:S(2)}, u32[]{:S(2)}) collective-permute-start(f32[16,256]{1,0:T(8,128)S(1)} %get-tuple-element.59), channel_id=1, source_target_pairs={{16,0},{32,16},{48,32},{64,48},{80,64},{96,80},{112,96},{128,112},... | collective-permute-start | bytes 49160 | tf_op jit(solution)/shard_map/ppermute | solution.py:499
  266.2 21.3 %all-to-all-start.11 = ((f32[16,8,128]{2,1,0:T(8,128)}), f32[16,8,128]{2,1,0:T(8,128)S(1)}, u32[]{:S(2)}, u32[]{:S(2)}) async-start(f32[16,8,128]{2,1,0:T(8,128)} %get-tuple-element.61), calls=%async_computation.11 | async-start | bytes 131072 | tf_op jit(solution)/shard_map/all_to_all | solution.py:494
  275.6 4.3 %collective-permute-start.6 = (f32[16,256]{1,0:T(8,128)S(1)}, f32[16,256]{1,0:T(8,128)S(1)}, u32[]{:S(2)}, u32[]{:S(2)}) collective-permute-start(f32[16,256]{1,0:T(8,128)S(1)} %get-tuple-element.62), channel_id=1, source_target_pairs={{0,16},{16,32},{32,48},{48,64},{64,80},{80,96},{96,112},{112,128},... | collective-permute-start | bytes 49160 | tf_op jit(solution)/shard_map/ppermute | solution.py:498
  277.8 5.4 %collective-permute-start.7 = (f32[16,256]{1,0:T(8,128)S(1)}, f32[16,256]{1,0:T(8,128)S(1)}, u32[]{:S(2)}, u32[]{:S(2)}) collective-permute-start(f32[16,256]{1,0:T(8,128)S(1)} %get-tuple-element.63), channel_id=1, source_target_pairs={{16,0},{32,16},{48,32},{64,48},{80,64},{96,80},{112,96},{128,112},... | collective-permute-start | bytes 49160 | tf_op jit(solution)/shard_map/ppermute | solution.py:499
  305.3 22.1 %all-to-all-start.13 = ((bf16[16,16,384]{2,1,0:T(8,128)(2,1)}), bf16[16,16,384]{2,1,0:T(8,128)(2,1)S(1)}, u32[]{:S(2)}, u32[]{:S(2)}) async-start(bf16[16,16,384]{2,1,0:T(8,128)(2,1)} %shard_map.137), calls=%async_computation.13 | async-start | bytes 393216 | tf_op jit(solution)/shard_map/all_to_all | solution.py:494
  370.6 15.6 %all-to-all-start.16 = ((f32[16,8,128]{2,1,0:T(8,128)}), f32[16,8,128]{2,1,0:T(8,128)S(1)}, u32[]{:S(2)}, u32[]{:S(2)}) async-start(f32[16,8,128]{2,1,0:T(8,128)} %get-tuple-element.72), calls=%async_computation.16 | async-start | bytes 131072 | tf_op jit(solution)/shard_map/all_to_all | solution.py:494
  374.6 5.9 %collective-permute-start.8 = (f32[16,256]{1,0:T(8,128)S(1)}, f32[16,256]{1,0:T(8,128)S(1)}, u32[]{:S(2)}, u32[]{:S(2)}) collective-permute-start(f32[16,256]{1,0:T(8,128)S(1)} %get-tuple-element.73), channel_id=1, source_target_pairs={{0,16},{16,32},{32,48},{48,64},{64,80},{80,96},{96,112},{112,128},... | collective-permute-start | bytes 49160 | tf_op jit(solution)/shard_map/ppermute | solution.py:498
  378.6 5.4 %collective-permute-start.9 = (f32[16,256]{1,0:T(8,128)S(1)}, f32[16,256]{1,0:T(8,128)S(1)}, u32[]{:S(2)}, u32[]{:S(2)}) collective-permute-start(f32[16,256]{1,0:T(8,128)S(1)} %get-tuple-element.74), channel_id=1, source_target_pairs={{16,0},{32,16},{48,32},{64,48},{80,64},{96,80},{112,96},{128,112},... | collective-permute-start | bytes 49160 | tf_op jit(solution)/shard_map/ppermute | solution.py:499

commit v3 on v2

--- a/solution.py
+++ b/solution.py
@@ -81,6 +81,23 @@
     for copy in copies:
         copy.start()
     return copies
+
+
+class Step:
+    def __init__(self, copy, later):
+        self.copy, self.later = copy, later
+
+    def wait(self):
+        self.copy.wait()
+        if self.later is not None:
+            self.later.start()
+
+
+def flowing(pairs, sems):
+    copies = [pltpu.make_async_copy(src, dst, sems.at[i]) for i, (src, dst) in enumerate(pairs)]
+    for copy in copies[:2]:
+        copy.start()
+    return [Step(copy, later) for copy, later in zip(copies, copies[2:] + [None, None])]
 
 
 def live_mask(counts):
@@ -243,7 +260,7 @@
 
 
 def k_load(recv, oh_hbm, msg, oh, sems):
-    waits = started([(oh_hbm.at[i], oh.at[i]) for i in range(LOAD_PARTS)], sems)
+    waits = flowing([(oh_hbm.at[i], oh.at[i]) for i in range(LOAD_PARTS)], sems)
     terms = [recv[g].astype(F32)[:, :OWN] for g in range(N_GRP)]
     terms = jnp.concatenate(terms, axis=1).astype(BF16)
     load = jnp.zeros((LOADS, ROWS), F32)
@@ -333,7 +350,7 @@
 
 
 def pick_starts(oh_hbm, oh, sems):
-    return started([(oh_hbm.at[i], oh.at[i]) for i in range(PICK_PARTS)], sems)
+    return flowing([(oh_hbm.at[i], oh.at[i]) for i in range(PICK_PARTS)], sems)
 
 
 def k_pick(recv, oh_hbm, msg, oh, sems):
@@ -382,7 +399,7 @@
 
 def k_smooth(y, peers, lo, hi, counts, schur_hbm, r_out, m_out, peers_out, below, above, schur, sems):
     rows = [slice(SLAB * i, SLAB * (i + 1)) for i in range(FIELD_PARTS)]
-    waits = started([(schur_hbm.at[part, :], schur.at[part, :]) for part in rows], sems)
+    waits = flowing([(schur_hbm.at[part, :], schur.at[part, :]) for part in rows], sems)
     r = jump(y, peers, lo, hi, counts, 1.0)
     r_out[...] = r
     r = halves(r)
@@ -425,7 +442,7 @@
     y, peers, lo, hi, counts, sums, r0, p0, q0, w0, u_hbm, mult_out, res_out, u, sems
 ):
     rows = [slice(SLAB * i, SLAB * (i + 1)) for i in range(FIELD_PARTS)]
-    waits = started([(u_hbm.at[part, :], u.at[part, :]) for part in rows], sems)
+    waits = flowing([(u_hbm.at[part, :], u.at[part, :]) for part in rows], sems)
     z = jump(y, peers, lo, hi, counts, 1.0)
     rp, pq, rw, qw, local, coarse = (sums[:, i : i + 1] for i in range(6))
     p, q, w = p0[...], q0[...], w0[...]

time: 395 us -> 403 us (1.020)
  Pallas kernels: 71.4 us -> 79.3 us
    pallas_call x20, Pallas kernels: 43.5 us -> 51.5 us  [call(): pl.pallas_call(body, out_shape=[pltpu.HBM(s, d) if i in out_hbm else jax....]
where the time goes in v3:
time: 403 us; the launch traced here: 400 us
  blocking collectives  125 us (31%)
  starting transfers between devices  110 us (27%)
  Pallas kernels  79.3 us (20%)
  waiting for transfers between devices  70.6 us (18%)
  matrix products  9.52 us (2%)
  local copies, waits for them, and re-layouts  4.04 us (1%)
    all_to_all x6, blocking collectives, over(): return lax.all_to_all(x, axis, split_axis=0, concat_axis=0, tiled=True)  125 us
    all_to_all x11, starting transfers between devices, over(): return lax.all_to_all(x, axis, split_axis=0, concat_axis=0, tiled=True)  80.7 us
    all_to_all x11, waiting for transfers between devices, over(): return lax.all_to_all(x, axis, split_axis=0, concat_axis=0, tiled=True)  57.1 us
    pallas_call x20, Pallas kernels, call(): pl.pallas_call(body, out_shape=[pltpu.HBM(s, d) if i in out_hbm else jax....  51.5 us
    pallas_call x2, Pallas kernels, permuted(): pl.pallas_call(k_permute, grid=(SUBS,), out_shape=jax.ShapeDtypeStruct((L...  27.9 us
    ppermute x5, starting transfers between devices, exchange(): up = lax.ppermute(above, 'grp', [(i, i + 1) for i in range(N_GRP - 1)])  19.1 us
    ppermute x5, waiting for transfers between devices, exchange(): down = lax.ppermute(below, 'grp', [(i + 1, i) for i in range(N_GRP - 1)])  13.5 us
    ppermute x5, starting transfers between devices, exchange(): down = lax.ppermute(below, 'grp', [(i + 1, i) for i in range(N_GRP - 1)])  9.97 us
  transfers between devices with their start and end apart: 21, of which 13 were waited for; matrix products, arithmetic and copies ran while one was open for 2% of the time, Pallas kernels for 8%

profile of v3, /device:TPU:1, one launch (start us, length us, event | category | flops | bytes accessed | tf_op | source)
XLA Modules:
  0.0 400.1 jit_solution(1005810103144349793)
XLA Ops:
  2.1 6.1 %shard_map.122 = (bf16[1536,1536]{1,0:T(8,128)(2,1)}, bf16[128,1536]{1,0:T(8,128)(2,1)S(1)}, bf16[16,1536]{1,0:T(8,128)(2,1)S(1)}, bf16[32,24,512]{2,1,0:T(8,128)(2,1)}) custom-call(f32[16,6144]{1,0:T(8,128)} %bv_hbm.1, s32[1,384]{1,0:T(1,128)} %bitcast.32, bf16[3,512,128]{2,1,0:T(8,128)(2,1)} %bitcast.28, bf16[16,1536]{1,0:T(8,128)(2,1)} %bitcast.30, ...), custom_call_target="tpu_custom_call" | custom-call | tf_op jit(solution)/shard_map/pallas_call | solution.py:66
  8.2 10.4 %all-to-all-start = ((bf16[32,24,512]{2,1,0:T(8,128)(2,1)}), bf16[32,24,512]{2,1,0:T(8,128)(2,1)S(1)}, u32[]{:S(2)}, u32[]{:S(2)}) async-start(bf16[32,24,512]{2,1,0:T(8,128)(2,1)} %get-tuple-element.40), calls=%async_computation | async-start | bytes 1572864 | tf_op jit(solution)/shard_map/all_to_all | solution.py:511
  18.7 14.3 %all-to-all-done.recv = bf16[32,24,512]{2,1,0:T(8,128)(2,1)S(1)} async-done(((bf16[32,24,512]{2,1,0:T(8,128)(2,1)}), bf16[32,24,512]{2,1,0:T(8,128)(2,1)S(1)}, u32[]{:S(2)}, u32[]{:S(2)}) %all-to-all-start) | async-done | bytes 786464 | tf_op jit(solution)/shard_map/all_to_all | solution.py:511
  33.0 1.5 shard_map.123
  34.5 26.0 %all_to_all.85.recv = bf16[16,56,128]{2,1,0:T(8,128)(2,1)S(1)} all-to-all(bf16[16,56,128]{2,1,0:T(8,128)(2,1)S(1)} %get-tuple-element.41), channel_id=1, replica_groups=mesh['grp'=32,'sub'=16] {'sub'}, dimensions={0} | all-to-all | bytes 458752 | tf_op jit(solution)/shard_map/all_to_all | solution.py:511
  60.5 1.2 shard_map.124
  61.7 8.4 %all-to-all-start.2 = ((bf16[32,16,768]{2,1,0:T(8,128)(2,1)}), bf16[32,16,768]{2,1,0:T(8,128)(2,1)S(1)}, u32[]{:S(2)}, u32[]{:S(2)}) async-start(bf16[32,16,768]{2,1,0:T(8,128)(2,1)} %shard_map.124), calls=%async_computation.2 | async-start | bytes 1572864 | tf_op jit(solution)/shard_map/all_to_all | solution.py:511
  70.1 1.4 copy-done
  71.5 13.9 %k_permute.2 = bf16[1536,1536]{1,0:T(8,128)(2,1)} custom-call(bf16[1536,1536]{1,0:T(8,128)(2,1)} %get-tuple-element.45.u.u_hbm, bf16[3,512,512]{2,1,0:T(8,128)(2,1)S(1)} %bitcast.20), custom_call_target="tpu_custom_call" | custom-call | tf_op jit(solution)/shard_map/k_permute/pallas_call | solution.py:477
  85.5 2.0 shard_map.125.oh_hbm
  87.5 3.1 shard_map.126
  90.7 5.6 %all-to-all-start.3 = ((bf16[16,16,128]{2,1,0:T(8,128)(2,1)}), bf16[16,16,128]{2,1,0:T(8,128)(2,1)S(1)}, u32[]{:S(2)}, u32[]{:S(2)}) async-start(bf16[16,16,128]{2,1,0:T(8,128)(2,1)} %shard_map.126), calls=%async_computation.3 | async-start | bytes 131072 | tf_op jit(solution)/shard_map/all_to_all | solution.py:511
  96.3 3.1 fusion.local
  99.3 8.5 %all-to-all-done.3.recv = bf16[16,16,128]{2,1,0:T(8,128)(2,1)S(1)} async-done(((bf16[16,16,128]{2,1,0:T(8,128)(2,1)}), bf16[16,16,128]{2,1,0:T(8,128)(2,1)S(1)}, u32[]{:S(2)}, u32[]{:S(2)}) %all-to-all-start.3) | async-done | bytes 65568 | tf_op jit(solution)/shard_map/all_to_all | solution.py:511
  110.5 4.0 all-to-all-start.4
  114.5 4.9 %collective-permute-start = (f32[16,256]{1,0:T(8,128)}, f32[16,256]{1,0:T(8,128)S(1)}, u32[]{:S(2)}, u32[]{:S(2)}) collective-permute-start(f32[16,256]{1,0:T(8,128)} %get-tuple-element.48), channel_id=1, source_target_pairs={{0,16},{16,32},{32,48},{48,64},{64,80},{80,96},{96,112},{112,128},... | collective-permute-start | bytes 49160 | tf_op jit(solution)/shard_map/ppermute | solution.py:515
  119.4 2.1 collective-permute-start.1
  121.5 13.9 %k_permute.3.schur_hbm = bf16[1536,1536]{1,0:T(8,128)(2,1)} custom-call(bf16[1536,1536]{1,0:T(8,128)(2,1)} %get-tuple-element.45.u.u_hbm, bf16[3,512,512]{2,1,0:T(8,128)(2,1)S(1)} %bitcast.21), custom_call_target="tpu_custom_call" | custom-call | tf_op jit(solution)/shard_map/k_permute/pallas_call | solution.py:477
  135.5 5.2 %shard_map.128 = (f32[16,1536]{1,0:T(8,128)S(1)}, f32[16,1536]{1,0:T(8,128)S(1)}, f32[16,8,128]{2,1,0:T(8,128)}, f32[16,256]{1,0:T(8,128)S(1)}, f32[16,256]{1,0:T(8,128)S(1)}) custom-call(f32[16,1536]{1,0:T(8,128)S(1)} %copy-done.3, f32[16,8,128]{2,1,0:T(8,128)S(1)} %all-to-all-done.4.peers, f32[16,256]{1,0:T(8,128)S(1)} %collective-permute-done.lo, ...), custom_call_target="tpu_custom_call" | custom-call | tf_op jit(solution)/shard_map/pallas_call | solution.py:66
  140.7 11.7 %all-to-all-start.5 = ((f32[16,8,128]{2,1,0:T(8,128)}), f32[16,8,128]{2,1,0:T(8,128)S(1)}, u32[]{:S(2)}, u32[]{:S(2)}) async-start(f32[16,8,128]{2,1,0:T(8,128)} %get-tuple-element.51), calls=%async_computation.5 | async-start | bytes 131072 | tf_op jit(solution)/shard_map/all_to_all | solution.py:511
  152.4 3.9 collective-permute-start.2
  156.3 1.9 collective-permute-start.3
  158.3 3.4 collective-permute-done.3.hi
  161.7 2.4 all-to-all-done.5.peers
  164.0 1.5 shard_map.129
  165.5 8.9 %all-to-all-start.6 = ((bf16[32,16,128]{2,1,0:T(8,128)(2,1)}), bf16[32,16,128]{2,1,0:T(8,128)(2,1)S(1)}, u32[]{:S(2)}, u32[]{:S(2)}) async-start(bf16[32,16,128]{2,1,0:T(8,128)(2,1)} %get-tuple-element.54), calls=%async_computation.6 | async-start | bytes 262144 | tf_op jit(solution)/shard_map/all_to_all | solution.py:511
  174.4 2.0 shard_map.130.oh_hbm
  176.4 5.6 %all-to-all-done.6.recv = bf16[32,16,128]{2,1,0:T(8,128)(2,1)S(1)} async-done(((bf16[32,16,128]{2,1,0:T(8,128)(2,1)}), bf16[32,16,128]{2,1,0:T(8,128)(2,1)S(1)}, u32[]{:S(2)}, u32[]{:S(2)}) %all-to-all-start.6) | async-done | bytes 131104 | tf_op jit(solution)/shard_map/all_to_all | solution.py:511
  182.0 3.3 shard_map.131
  185.3 23.2 %all_to_all.86.recv = bf16[16,16,384]{2,1,0:T(8,128)(2,1)S(1)} all-to-all(bf16[16,16,384]{2,1,0:T(8,128)(2,1)S(1)} %shard_map.131), channel_id=1, replica_groups=mesh['grp'=32,'sub'=16] {'sub'}, dimensions={0} | all-to-all | bytes 393216 | tf_op jit(solution)/shard_map/all_to_all | solution.py:511
  208.9 21.5 %all_to_all.87.recv = bf16[32,16,768]{2,1,0:T(8,128)(2,1)S(1)} all-to-all(bf16[32,16,768]{2,1,0:T(8,128)(2,1)S(1)} %shard_map.132), channel_id=1, replica_groups=mesh['grp'=32,'sub'=16] {'grp'}, dimensions={0} | all-to-all | bytes 1572864 | tf_op jit(solution)/shard_map/all_to_all | solution.py:511
  230.4 3.1 shard_map.133
  233.5 5.3 %all-to-all-start.9 = ((bf16[16,16,128]{2,1,0:T(8,128)(2,1)}), bf16[16,16,128]{2,1,0:T(8,128)(2,1)S(1)}, u32[]{:S(2)}, u32[]{:S(2)}) async-start(bf16[16,16,128]{2,1,0:T(8,128)(2,1)} %shard_map.133), calls=%async_computation.9 | async-start | bytes 131072 | tf_op jit(solution)/shard_map/all_to_all | solution.py:511
  238.8 3.2 fusion.1.local
  242.0 8.3 %all-to-all-done.9.recv = bf16[16,16,128]{2,1,0:T(8,128)(2,1)S(1)} async-done(((bf16[16,16,128]{2,1,0:T(8,128)(2,1)}), bf16[16,16,128]{2,1,0:T(8,128)(2,1)S(1)}, u32[]{:S(2)}, u32[]{:S(2)}) %all-to-all-start.9) | async-done | bytes 65568 | tf_op jit(solution)/shard_map/all_to_all | solution.py:511
  250.3 0.9 shard_map.134
  251.2 3.8 all-to-all-start.10
  255.0 4.2 %collective-permute-start.4 = (f32[16,256]{1,0:T(8,128)S(1)}, f32[16,256]{1,0:T(8,128)S(1)}, u32[]{:S(2)}, u32[]{:S(2)}) collective-permute-start(f32[16,256]{1,0:T(8,128)S(1)} %get-tuple-element.58), channel_id=1, source_target_pairs={{0,16},{16,32},{32,48},{48,64},{64,80},{80,96},{96,112},{112,128},... | collective-permute-start | bytes 49160 | tf_op jit(solution)/shard_map/ppermute | solution.py:515
  259.2 1.9 collective-permute-start.5
  261.2 3.4 collective-permute-done.5.hi
  264.6 2.0 all-to-all-done.10.peers
  266.6 5.2 %shard_map.135 = (f32[16,1536]{1,0:T(8,128)S(1)}, f32[16,1536]{1,0:T(8,128)S(1)}, f32[16,8,128]{2,1,0:T(8,128)}, f32[16,256]{1,0:T(8,128)S(1)}, f32[16,256]{1,0:T(8,128)S(1)}) custom-call(f32[16,1536]{1,0:T(8,128)S(1)} %get-tuple-element.56.y, f32[16,8,128]{2,1,0:T(8,128)S(1)} %all-to-all-done.10.peers, f32[16,256]{1,0:T(8,128)S(1)} %collective-permute-done.4.lo, ...), custom_call_target="tpu_custom_call" | custom-call | tf_op jit(solution)/shard_map/pallas_call | solution.py:66
  271.9 9.3 %all-to-all-start.11 = ((f32[16,8,128]{2,1,0:T(8,128)}), f32[16,8,128]{2,1,0:T(8,128)S(1)}, u32[]{:S(2)}, u32[]{:S(2)}) async-start(f32[16,8,128]{2,1,0:T(8,128)} %get-tuple-element.61), calls=%async_computation.11 | async-start | bytes 131072 | tf_op jit(solution)/shard_map/all_to_all | solution.py:511
  281.2 2.2 collective-permute-start.6
  283.4 2.1 collective-permute-start.7
  285.6 3.2 collective-permute-done.7.hi
  288.8 4.4 %all-to-all-done.11.peers = f32[16,8,128]{2,1,0:T(8,128)S(1)} async-done(((f32[16,8,128]{2,1,0:T(8,128)}), f32[16,8,128]{2,1,0:T(8,128)S(1)}, u32[]{:S(2)}, u32[]{:S(2)}) %all-to-all-start.11) | async-done | bytes 65568 | tf_op jit(solution)/shard_map/all_to_all | solution.py:511
  293.2 0.8 shard_map.136
  294.0 14.4 %all_to_all.88.recv = bf16[32,16,128]{2,1,0:T(8,128)(2,1)S(1)} all-to-all(bf16[32,16,128]{2,1,0:T(8,128)(2,1)S(1)} %get-tuple-element.67), channel_id=1, replica_groups=mesh['grp'=32,'sub'=16] {'grp'}, dimensions={0} | all-to-all | bytes 262144 | tf_op jit(solution)/shard_map/all_to_all | solution.py:511
  308.4 4.0 %shard_map.137 = bf16[16,16,384]{2,1,0:T(8,128)(2,1)} custom-call(bf16[32,16,128]{2,1,0:T(8,128)(2,1)S(1)} %all_to_all.88.recv, bf16[6,384,384]{2,1,0:T(8,128)(2,1)} %shard_map.130.oh_hbm), custom_call_target="tpu_custom_call" | custom-call | tf_op jit(solution)/shard_map/pallas_call | solution.py:66
  312.4 9.5 %all-to-all-start.13 = ((bf16[16,16,384]{2,1,0:T(8,128)(2,1)}), bf16[16,16,384]{2,1,0:T(8,128)(2,1)S(1)}, u32[]{:S(2)}, u32[]{:S(2)}) async-start(bf16[16,16,384]{2,1,0:T(8,128)(2,1)} %shard_map.137), calls=%async_computation.13 | async-start | bytes 393216 | tf_op jit(solution)/shard_map/all_to_all | solution.py:511
  321.9 3.2 fusion.2.local
  325.1 9.4 %all-to-all-done.13.recv = bf16[16,16,384]{2,1,0:T(8,128)(2,1)S(1)} async-done(((bf16[16,16,384]{2,1,0:T(8,128)(2,1)}), bf16[16,16,384]{2,1,0:T(8,128)(2,1)S(1)}, u32[]{:S(2)}, u32[]{:S(2)}) %all-to-all-start.13) | async-done | bytes 196640 | tf_op jit(solution)/shard_map/all_to_all | solution.py:511
  334.5 0.8 shard_map.138
  335.3 22.9 %all_to_all.89.recv = bf16[32,16,896]{2,1,0:T(8,128)(2,1)S(1)} all-to-all(bf16[32,16,896]{2,1,0:T(8,128)(2,1)S(1)} %shard_map.138), channel_id=1, replica_groups=mesh['grp'=32,'sub'=16] {'grp'}, dimensions={0} | all-to-all | bytes 1835008 | tf_op jit(solution)/shard_map/all_to_all | solution.py:511
  358.3 2.6 shard_map.139
  360.9 16.6 %all_to_all.90.recv = bf16[16,16,128]{2,1,0:T(8,128)(2,1)S(1)} all-to-all(bf16[16,16,128]{2,1,0:T(8,128)(2,1)S(1)} %shard_map.139), channel_id=1, replica_groups=mesh['grp'=32,'sub'=16] {'sub'}, dimensions={0} | all-to-all | bytes 131072 | tf_op jit(solution)/shard_map/all_to_all | solution.py:511
  377.5 0.9 shard_map.140
  378.4 4.0 all-to-all-start.16
  382.4 4.0 collective-permute-start.8
  386.3 1.9 collective-permute-start.9
  388.3 3.4 collective-permute-done.9.hi
  391.7 2.2 all-to-all-done.16.peers
  393.9 6.0 %shard_map.141 = (f32[16,1536]{1,0:T(8,128)}, f32[16,1536]{1,0:T(8,128)}) custom-call(f32[16,1536]{1,0:T(8,128)S(1)} %get-tuple-element.71.y, f32[16,8,128]{2,1,0:T(8,128)S(1)} %all-to-all-done.16.peers, f32[16,256]{1,0:T(8,128)S(1)} %collective-permute-done.8.lo, f32[16,256]{1,0:T(8,128)S(1)} %collective-permute-done.9.hi, s32[1,18]{1,0:T(1,128)S(1)} %bitcast.27, ...), custom_call_target="tpu_custom_call" | custom-call | tf_op jit(solution)/shard_map/pallas_call | solution.py:66
  (33 shorter events, 4.5 us)
Async XLA Ops:
  1.4 0.7 copy-start.5
  8.2 24.8 %all-to-all-start = ((bf16[32,24,512]{2,1,0:T(8,128)(2,1)}), bf16[32,24,512]{2,1,0:T(8,128)(2,1)S(1)}, u32[]{:S(2)}, u32[]{:S(2)}) async-start(bf16[32,24,512]{2,1,0:T(8,128)(2,1)} %get-tuple-element.40), calls=%async_computation | async-start | bytes 1572864 | tf_op jit(solution)/shard_map/all_to_all | solution.py:511
  18.7 66.8 %copy-start.7 = (s32[1,2]{1,0:T(1,128)}, s32[1,2]{1,0:T(1,128)S(1)}, u32[]{:S(2)}) copy-start(s32[1,2]{1,0:T(1,128)S(1)} %add_bitcast_fusion.where) | copy-start | bytes 28
  61.7 25.8 %all-to-all-start.2 = ((bf16[32,16,768]{2,1,0:T(8,128)(2,1)}), bf16[32,16,768]{2,1,0:T(8,128)(2,1)S(1)}, u32[]{:S(2)}, u32[]{:S(2)}) async-start(bf16[32,16,768]{2,1,0:T(8,128)(2,1)} %shard_map.124), calls=%async_computation.2 | async-start | bytes 1572864 | tf_op jit(solution)/shard_map/all_to_all | solution.py:511
  70.1 1.4 copy-start
  90.6 30.8 %copy-start.1 = (bf16[1,1,3,512,512]{4,3,2,1,0:T(8,128)(2,1)S(1)}, bf16[1,1,3,512,512]{4,3,2,1,0:T(8,128)(2,1)}, u32[]{:S(2)}) copy-start(bf16[1,1,3,512,512]{4,3,2,1,0:T(8,128)(2,1)} %param.16) | copy-start | bytes 4718596
  90.7 17.2 %all-to-all-start.3 = ((bf16[16,16,128]{2,1,0:T(8,128)(2,1)}), bf16[16,16,128]{2,1,0:T(8,128)(2,1)S(1)}, u32[]{:S(2)}, u32[]{:S(2)}) async-start(bf16[16,16,128]{2,1,0:T(8,128)(2,1)} %shard_map.126), calls=%async_computation.3 | async-start | bytes 131072 | tf_op jit(solution)/shard_map/all_to_all | solution.py:511
  108.7 0.6 copy-start.2
  109.3 0.6 copy-start.4
  109.9 0.6 copy-start.9
  110.5 24.9 %all-to-all-start.4 = ((f32[16,8,128]{2,1,0:T(8,128)}), f32[16,8,128]{2,1,0:T(8,128)S(1)}, u32[]{:S(2)}, u32[]{:S(2)}) async-start(f32[16,8,128]{2,1,0:T(8,128)} %copy-done.4), calls=%async_computation.4 | async-start | bytes 131072 | tf_op jit(solution)/shard_map/all_to_all | solution.py:511
  114.5 20.9 %collective-permute-start = (f32[16,256]{1,0:T(8,128)}, f32[16,256]{1,0:T(8,128)S(1)}, u32[]{:S(2)}, u32[]{:S(2)}) collective-permute-start(f32[16,256]{1,0:T(8,128)} %get-tuple-element.48), channel_id=1, source_target_pairs={{0,16},{16,32},{32,48},{48,64},{64,80},{80,96},{96,112},{112,128},... | collective-permute-start | bytes 49160 | tf_op jit(solution)/shard_map/ppermute | solution.py:515
  119.4 16.1 %collective-permute-start.1 = (f32[16,256]{1,0:T(8,128)}, f32[16,256]{1,0:T(8,128)S(1)}, u32[]{:S(2)}, u32[]{:S(2)}) collective-permute-start(f32[16,256]{1,0:T(8,128)} %copy-done.9), channel_id=1, source_target_pairs={{16,0},{32,16},{48,32},{64,48},{80,64},{96,80},{112,96},{128,112},... | collective-permute-start | bytes 49160 | tf_op jit(solution)/shard_map/ppermute | solution.py:516
  121.5 14.0 %copy-start.3 = (f32[16,1536]{1,0:T(8,128)S(1)}, f32[16,1536]{1,0:T(8,128)}, u32[]{:S(2)}) copy-start(f32[16,1536]{1,0:T(8,128)} %copy-done.2) | copy-start | bytes 294916
  121.5 14.0 %copy-start.6 = (s32[1,1,18]{2,1,0:T(1,128)S(1)}, s32[1,1,18]{2,1,0:T(1,128)}, u32[]{:S(2)}) copy-start(s32[1,1,18]{2,1,0:T(1,128)} %param.20) | copy-start | bytes 220
  135.4 39.0 %copy-start.8 = (s32[1,2]{1,0:T(1,128)S(1)}, s32[1,2]{1,0:T(1,128)}, u32[]{:S(2)}) copy-start(s32[1,2]{1,0:T(1,128)} %copy-done.7) | copy-start | bytes 28
  140.7 23.3 %all-to-all-start.5 = ((f32[16,8,128]{2,1,0:T(8,128)}), f32[16,8,128]{2,1,0:T(8,128)S(1)}, u32[]{:S(2)}, u32[]{:S(2)}) async-start(f32[16,8,128]{2,1,0:T(8,128)} %get-tuple-element.51), calls=%async_computation.5 | async-start | bytes 131072 | tf_op jit(solution)/shard_map/all_to_all | solution.py:511
  152.4 5.9 %collective-permute-start.2 = (f32[16,256]{1,0:T(8,128)S(1)}, f32[16,256]{1,0:T(8,128)S(1)}, u32[]{:S(2)}, u32[]{:S(2)}) collective-permute-start(f32[16,256]{1,0:T(8,128)S(1)} %get-tuple-element.52), channel_id=1, source_target_pairs={{0,16},{16,32},{32,48},{48,64},{64,80},{80,96},{96,112},{112,128},... | collective-permute-start | bytes 49160 | tf_op jit(solution)/shard_map/ppermute | solution.py:515
  156.3 5.4 %collective-permute-start.3 = (f32[16,256]{1,0:T(8,128)S(1)}, f32[16,256]{1,0:T(8,128)S(1)}, u32[]{:S(2)}, u32[]{:S(2)}) collective-permute-start(f32[16,256]{1,0:T(8,128)S(1)} %get-tuple-element.53), channel_id=1, source_target_pairs={{16,0},{32,16},{48,32},{64,48},{80,64},{96,80},{112,96},{128,112},... | collective-permute-start | bytes 49160 | tf_op jit(solution)/shard_map/ppermute | solution.py:516
  165.5 16.5 %all-to-all-start.6 = ((bf16[32,16,128]{2,1,0:T(8,128)(2,1)}), bf16[32,16,128]{2,1,0:T(8,128)(2,1)S(1)}, u32[]{:S(2)}, u32[]{:S(2)}) async-start(bf16[32,16,128]{2,1,0:T(8,128)(2,1)} %get-tuple-element.54), calls=%async_computation.6 | async-start | bytes 262144 | tf_op jit(solution)/shard_map/all_to_all | solution.py:511
  233.5 16.8 %all-to-all-start.9 = ((bf16[16,16,128]{2,1,0:T(8,128)(2,1)}), bf16[16,16,128]{2,1,0:T(8,128)(2,1)S(1)}, u32[]{:S(2)}, u32[]{:S(2)}) async-start(bf16[16,16,128]{2,1,0:T(8,128)(2,1)} %shard_map.133), calls=%async_computation.9 | async-start | bytes 131072 | tf_op jit(solution)/shard_map/all_to_all | solution.py:511
  251.2 15.4 %all-to-all-start.10 = ((f32[16,8,128]{2,1,0:T(8,128)}), f32[16,8,128]{2,1,0:T(8,128)S(1)}, u32[]{:S(2)}, u32[]{:S(2)}) async-start(f32[16,8,128]{2,1,0:T(8,128)} %get-tuple-element.57), calls=%async_computation.10 | async-start | bytes 131072 | tf_op jit(solution)/shard_map/all_to_all | solution.py:511
  255.0 6.1 %collective-permute-start.4 = (f32[16,256]{1,0:T(8,128)S(1)}, f32[16,256]{1,0:T(8,128)S(1)}, u32[]{:S(2)}, u32[]{:S(2)}) collective-permute-start(f32[16,256]{1,0:T(8,128)S(1)} %get-tuple-element.58), channel_id=1, source_target_pairs={{0,16},{16,32},{32,48},{48,64},{64,80},{80,96},{96,112},{112,128},... | collective-permute-start | bytes 49160 | tf_op jit(solution)/shard_map/ppermute | solution.py:515
  259.2 5.4 %collective-permute-start.5 = (f32[16,256]{1,0:T(8,128)S(1)}, f32[16,256]{1,0:T(8,128)S(1)}, u32[]{:S(2)}, u32[]{:S(2)}) collective-permute-start(f32[16,256]{1,0:T(8,128)S(1)} %get-tuple-element.59), channel_id=1, source_target_pairs={{16,0},{32,16},{48,32},{64,48},{80,64},{96,80},{112,96},{128,112},... | collective-permute-start | bytes 49160 | tf_op jit(solution)/shard_map/ppermute | solution.py:516
  271.9 21.3 %all-to-all-start.11 = ((f32[16,8,128]{2,1,0:T(8,128)}), f32[16,8,128]{2,1,0:T(8,128)S(1)}, u32[]{:S(2)}, u32[]{:S(2)}) async-start(f32[16,8,128]{2,1,0:T(8,128)} %get-tuple-element.61), calls=%async_computation.11 | async-start | bytes 131072 | tf_op jit(solution)/shard_map/all_to_all | solution.py:511
  281.2 4.3 %collective-permute-start.6 = (f32[16,256]{1,0:T(8,128)S(1)}, f32[16,256]{1,0:T(8,128)S(1)}, u32[]{:S(2)}, u32[]{:S(2)}) collective-permute-start(f32[16,256]{1,0:T(8,128)S(1)} %get-tuple-element.62), channel_id=1, source_target_pairs={{0,16},{16,32},{32,48},{48,64},{64,80},{80,96},{96,112},{112,128},... | collective-permute-start | bytes 49160 | tf_op jit(solution)/shard_map/ppermute | solution.py:515
  283.4 5.4 %collective-permute-start.7 = (f32[16,256]{1,0:T(8,128)S(1)}, f32[16,256]{1,0:T(8,128)S(1)}, u32[]{:S(2)}, u32[]{:S(2)}) collective-permute-start(f32[16,256]{1,0:T(8,128)S(1)} %get-tuple-element.63), channel_id=1, source_target_pairs={{16,0},{32,16},{48,32},{64,48},{80,64},{96,80},{112,96},{128,112},... | collective-permute-start | bytes 49160 | tf_op jit(solution)/shard_map/ppermute | solution.py:516
  312.4 22.1 %all-to-all-start.13 = ((bf16[16,16,384]{2,1,0:T(8,128)(2,1)}), bf16[16,16,384]{2,1,0:T(8,128)(2,1)S(1)}, u32[]{:S(2)}, u32[]{:S(2)}) async-start(bf16[16,16,384]{2,1,0:T(8,128)(2,1)} %shard_map.137), calls=%async_computation.13 | async-start | bytes 393216 | tf_op jit(solution)/shard_map/all_to_all | solution.py:511
  378.4 15.6 %all-to-all-start.16 = ((f32[16,8,128]{2,1,0:T(8,128)}), f32[16,8,128]{2,1,0:T(8,128)S(1)}, u32[]{:S(2)}, u32[]{:S(2)}) async-start(f32[16,8,128]{2,1,0:T(8,128)} %get-tuple-element.72), calls=%async_computation.16 | async-start | bytes 131072 | tf_op jit(solution)/shard_map/all_to_all | solution.py:511
  382.4 5.9 %collective-permute-start.8 = (f32[16,256]{1,0:T(8,128)S(1)}, f32[16,256]{1,0:T(8,128)S(1)}, u32[]{:S(2)}, u32[]{:S(2)}) collective-permute-start(f32[16,256]{1,0:T(8,128)S(1)} %get-tuple-element.73), channel_id=1, source_target_pairs={{0,16},{16,32},{32,48},{48,64},{64,80},{80,96},{96,112},{112,128},... | collective-permute-start | bytes 49160 | tf_op jit(solution)/shard_map/ppermute | solution.py:515
  386.3 5.4 %collective-permute-start.9 = (f32[16,256]{1,0:T(8,128)S(1)}, f32[16,256]{1,0:T(8,128)S(1)}, u32[]{:S(2)}, u32[]{:S(2)}) collective-permute-start(f32[16,256]{1,0:T(8,128)S(1)} %get-tuple-element.74), channel_id=1, source_target_pairs={{16,0},{32,16},{48,32},{64,48},{80,64},{96,80},{112,96},{128,112},... | collective-permute-start | bytes 49160 | tf_op jit(solution)/shard_map/ppermute | solution.py:516
